TPU v7x, 32 devices: a whole 2x2x4 slice. The times are simulated.
32 devices in a mesh: gx: 8 (over z, y), gy: 4 (over x, core).
Axes of the slice: x: 2, y: 2, z: 4, core: 2. Of those that a mesh axis runs over, the one named last changes fastest.
Arguments:
- charges: float32 [256, 128, 256], P('gx', 'gy'), may hold values from -6 to 6
- kernel_taps: float32 [3, 3, 21], replicated, may hold values from -1.08 to 1.08
Outputs:
- potential: float32 [256, 128, 256], P('gx', 'gy')
All inputs are finite; a program needn't handle non-finite values.
Results may differ from a plain program's by a relative error of at most 0.035.
Values sent between devices are 32-bit elements; how exact they have to be, the bound alone decides.
A program may use at most 128 MiB of HBM per device.

v0:
```python
import jax
import jax.numpy as jnp
from jax import lax
from jax.sharding import PartitionSpec as P

SPLINE = (0.125, 0.5, 0.75, 0.5, 0.125)


def padded_2(x, sides, width):
    for axis, dim in sides:
        peers, length = (lax.axis_size(axis), x.shape[dim])
        up = [(i, (i + 1) % peers) for i in range(peers)]
        down = [(j, i) for i, j in up]
        last = lax.slice_in_dim(x, length - width, length, axis=dim)
        first = lax.slice_in_dim(x, 0, width, axis=dim)
        before = lax.ppermute(last, axis, up)
        after = lax.ppermute(first, axis, down)
        x = jnp.concatenate([before, x, after], axis=dim)
    return x


def contract(formula, left, right):
    return jnp.einsum(formula, left, right, precision=lax.Precision.HIGHEST)


def grid_ids(count_rows, count_cols):
    row_ids = lax.broadcasted_iota(jnp.int32, (count_rows, count_cols), 0)
    col_ids = lax.broadcasted_iota(jnp.int32, (count_rows, count_cols), 1)
    return (row_ids, col_ids)


def spline_table(offsets):
    table = jnp.zeros(offsets.shape, jnp.float32)
    for position in range(5):
        table = table + SPLINE[position] * (offsets == position).astype(jnp.float32)
    return table


def band_taps(taps, count_rows, count_cols):
    row_ids, col_ids = grid_ids(count_rows, count_cols)
    offsets = col_ids - row_ids
    tap_count = taps.shape[1]
    inside = (offsets >= 0) & (offsets < tap_count)
    picked = jnp.take(taps, jnp.clip(offsets, 0, tap_count - 1), axis=1)
    return jnp.where(inside[None], picked, 0.0)


def cycle_taps(taps, length):
    tap_count = taps.shape[1]
    radius = tap_count // 2
    wrapped = (jnp.arange(tap_count, dtype=jnp.int32) - radius) % length
    onehot = (wrapped[:, None] == jnp.arange(length, dtype=jnp.int32)[None, :]).astype(jnp.float32)
    profile = jnp.dot(
        taps, onehot, preferred_element_type=jnp.float32, precision=lax.Precision.HIGHEST
    )
    row_ids, col_ids = grid_ids(length, length)
    return jnp.take(profile, (col_ids - row_ids) % length, axis=1)


def restrict_band(count_rows, count_cols, margin):
    row_ids, col_ids = grid_ids(count_rows, count_cols)
    return spline_table(col_ids - margin - 2 * row_ids + 2)


def restrict_cycle(length):
    row_ids, col_ids = grid_ids(length // 2, length)
    return spline_table((col_ids - 2 * row_ids + 2) % length)


def prolong_band(count_rows, count_cols):
    row_ids, col_ids = grid_ids(count_rows, count_cols)
    return spline_table(row_ids - 2 * col_ids + 4)


def prolong_cycle(count_rows, coarse_len, offset):
    row_ids, col_ids = grid_ids(count_rows, coarse_len)
    return spline_table((offset + row_ids - 2 * col_ids + 2) % (2 * coarse_len))


def body(charges, kernel_taps):
    radius = kernel_taps.shape[2] // 2
    margin = radius + 1
    term_count = kernel_taps.shape[1]
    rows_x, rows_y, cells_z = charges.shape
    half_x, half_y, half_z = (rows_x // 2, rows_y // 2, cells_z // 2)
    quarter_x, quarter_z = (rows_x // 4, cells_z // 4)
    count_x = lax.axis_size("gx")
    count_y = lax.axis_size("gy")
    wide_y = rows_y * count_y
    quarter_y = wide_y // 4
    taps_fine, taps_middle, taps_top = (kernel_taps[0], kernel_taps[1], kernel_taps[2])
    padded = padded_2(charges, (("gx", 0), ("gy", 1)), radius)
    across_x = band_taps(taps_fine, rows_x, rows_x + 2 * radius)
    across_y = band_taps(taps_fine, rows_y, rows_y + 2 * radius)
    across_z = cycle_taps(taps_fine, cells_z)
    direct_fine = jnp.zeros(charges.shape, jnp.float32)
    for member in range(term_count):
        sectioned = contract("mc,cyz->myz", across_x[member], padded)
        sectioned = contract("nc,mcz->mnz", across_y[member], sectioned)
        direct_fine = direct_fine + contract("mnz,wz->mnw", sectioned, across_z[member])
    coarse = contract("mc,cyz->myz", restrict_band(half_x, rows_x + 2 * radius, radius), padded)
    coarse = contract("nc,mcz->mnz", restrict_band(half_y, rows_y + 2 * radius, radius), coarse)
    coarse = contract("mnz,wz->mnw", coarse, restrict_cycle(cells_z))
    middle_x = band_taps(taps_middle, half_x + 2, half_x + 2 * margin)
    middle_z = cycle_taps(taps_middle, half_z)
    down_x = restrict_band(quarter_x, half_x + 2 * margin, margin)
    down_z = restrict_cycle(half_z)
    up_z = prolong_cycle(half_z, quarter_z, 0)
    rimmed = padded_2(coarse, (("gx", 0), ("gy", 1)), margin)
    middle_y = band_taps(taps_middle, half_y + 2, half_y + 2 * margin)
    direct_middle = jnp.zeros((half_x + 2, half_y + 2, half_z), jnp.float32)
    for member in range(term_count):
        sectioned = contract("mc,cyz->myz", middle_x[member], rimmed)
        sectioned = contract("nc,mcz->mnz", middle_y[member], sectioned)
        direct_middle = direct_middle + contract("mnz,wz->mnw", sectioned, middle_z[member])
    summit = contract("mc,cyz->myz", down_x, rimmed)
    summit = contract(
        "nc,mcz->mnz", restrict_band(half_y // 2, half_y + 2 * margin, margin), summit
    )
    summit = contract("mnz,wz->mnw", summit, down_z)
    lift_y = prolong_cycle(half_y + 2, quarter_y, lax.axis_index("gy") * half_y - 1)
    spread_y = prolong_band(rows_y, half_y + 2)
    top_y = cycle_taps(taps_top, quarter_y)
    top_z = cycle_taps(taps_top, quarter_z)
    full_x = quarter_x * count_x
    top_x = cycle_taps(taps_top, full_x)
    along_z = jnp.stack(
        [contract("mnz,wz->mnw", summit, top_z[member]) for member in range(term_count)]
    )
    portion = lax.all_to_all(along_z, "gy", split_axis=3, concat_axis=2, tiled=True)
    turned_yz = jnp.stack(
        [contract("nc,mcw->mnw", top_y[member], portion[member]) for member in range(term_count)]
    )
    up_x = prolong_cycle(2 * full_x, full_x, 0)
    portion = lax.all_to_all(turned_yz, "gx", split_axis=2, concat_axis=1, tiled=True)
    result = jnp.zeros(portion.shape[1:], jnp.float32)
    for member in range(term_count):
        result = result + contract("mc,cnw->mnw", top_x[member], portion[member])
    refined = contract("jm,mnw->jnw", up_x, result)
    rest_shape = refined.shape[1:]
    blocks = refined.reshape((count_x, half_x) + rest_shape)
    leading = jnp.roll(refined, 1, 0).reshape((count_x, half_x) + rest_shape)[:, :1]
    trailing = jnp.roll(refined, -1, 0).reshape((count_x, half_x) + rest_shape)[:, -1:]
    windows = jnp.concatenate([leading, blocks, trailing], axis=1)
    back_rows = lax.all_to_all(windows, "gx", split_axis=0, concat_axis=2, tiled=True)[0]
    returned = lax.all_gather(back_rows, "gy", axis=2, tiled=True)
    lifted = contract("jn,mnw->mjw", lift_y, returned)
    lifted = contract("mjz,wz->mjw", lifted, up_z)
    middle = direct_middle + lifted
    refined = contract("jm,myz->jyz", prolong_band(rows_x, half_x + 2), middle)
    refined = contract("jn,mnz->mjz", spread_y, refined)
    refined = contract("mjz,wz->mjw", refined, prolong_cycle(cells_z, half_z, 0))
    return direct_fine + refined


def solution(mesh):
    return jax.shard_map(
        body,
        mesh=mesh,
        in_specs=(P("gx", "gy", None), P()),
        out_specs=P("gx", "gy", None),
        check_vma=False,
    )
```

profile of v0, /device:TPU:0, one launch (start us, length us, event | category | flops | bytes accessed | tf_op | source)
XLA Modules:
  0.0 441.3 jit_solution(16400471521778791721)
XLA Ops:
  0.0 1.8 copy.40
  2.9 3.0 collective-permute-start
  5.9 3.0 collective-permute-start.1
  19.9 1.7 gather_fusion.4
  22.4 2.8 gather_fusion.2
  26.1 3.2 gather_fusion.3
  30.4 10.8 %gather_fusion.5 = f32[4096,3]{1,0:T(8,128)S(1)} fusion(f32[3,64]{0,1:T(8,128)S(1)} %copy.59, s32[4096]{0:T(1024)S(1)} %broadcast_clamp_fusion.1), kind=kCustom, calls=%fused_computation.2.clone | custom fusion | bytes 114688 | tf_op jit(solution)/shard_map/jit(_take)/gather | solution.py:57
  45.7 2.1 pad_maximum_fusion.4
  47.8 1.7 collective-permute-start.3
  49.8 54.8 %gather_fusion.1 = f32[16384,3]{1,0:T(8,128)} fusion(f32[3,128]{0,1:T(8,128)S(1)} %copy.53, s32[16384]{0:T(1024)S(1)} %copy-done.3), kind=kCustom, calls=%fused_computation.4 | custom fusion | bytes 458752 | tf_op jit(solution)/shard_map/jit(_take)/gather | solution.py:57
  104.6 5.2 %copy.54 = f32[128,128,3]{1,0,2:T(8,128)S(1)} copy(f32[128,128,3]{2,1,0:T(8,128)} %bitcast.268) | data formatting | bytes 393216 | tf_op jit(solution)/shard_map/jit(_take)/gather | solution.py:57
  109.9 217.0 %gather_fusion = f32[65536,3]{1,0:T(8,128)} fusion(f32[3,256]{0,1:T(8,128)S(1)} %copy.44, s32[65536]{0:T(1024)S(1)} %broadcast_clamp_fusion), kind=kCustom, calls=%fused_computation.3 | custom fusion | bytes 1835008 | tf_op jit(solution)/shard_map/jit(_take)/gather | solution.py:57
  326.9 18.9 %copy.87 = f32[256,256,3]{1,0,2:T(8,128)S(1)} copy(f32[256,256,3]{2,1,0:T(8,128)} %bitcast.267) | data formatting | bytes 1572864 | tf_op jit(solution)/shard_map/jit(_take)/gather | solution.py:57
  345.9 3.3 fusion.214
  351.0 5.2 %collective-permute-start.5 = (f32[11,16,128]{2,1,0:T(8,128)S(1)}, f32[11,16,128]{2,1,0:T(8,128)S(1)}, u32[]{:S(2)}, u32[]{:S(2)}) collective-permute-start(f32[11,16,128]{2,1,0:T(8,128)S(1)} %get-tuple-element.18), channel_id=1, source_target_pairs={{4,0},{8,4},{12,8},{16,12},{20,16},{24,20},{28,24},{0,28},{5,1},{9... | collective-permute-start | bytes 270344 | tf_op jit(solution)/shard_map/ppermute | solution.py:17
  356.2 3.3 fusion.181
  359.5 2.3 fusion.9
  361.8 3.3 fusion.180
  365.2 2.3 fusion.6
  369.6 3.5 fusion.182
  373.1 2.3 fusion.12
  375.6 1.7 collective-permute-start.7
  378.4 4.9 %collective-permute-done.6 = f32[38,11,128]{2,1,0:T(8,128)S(1)} collective-permute-done((f32[38,11,128]{2,1,0:T(8,128)S(1)}, f32[38,11,128]{2,1,0:T(8,128)S(1)}, u32[]{:S(2)}, u32[]{:S(2)}) %collective-permute-start.6) | collective-permute-done | bytes 214048 | tf_op jit(solution)/shard_map/ppermute | solution.py:16
  391.8 3.3 all-to-all-start
  395.8 3.3 all-to-all-done
  403.3 3.6 all-to-all-start.1
  407.3 6.3 %all-to-all-done.1 = f32[8,1,1536]{2,1,0:T(1,128)S(1)} async-done(((f32[8,1,1536]{2,1,0:T(1,128)}), f32[8,1,1536]{2,1,0:T(1,128)S(1)}, u32[]{:S(2)}, u32[]{:S(2)}) %all-to-all-start.1) | async-done | bytes 49184 | tf_op jit(solution)/shard_map/all_to_all | solution.py:135
  417.8 3.3 all-to-all-start.2
  421.5 6.3 %all-to-all-done.2 = f32[8,1,1152]{2,1,0:T(1,128)S(1)} async-done(((f32[8,1,1152]{2,1,0:T(1,128)}), f32[8,1,1152]{2,1,0:T(1,128)S(1)}, u32[]{:S(2)}, u32[]{:S(2)}) %all-to-all-start.2) | async-done | bytes 36896 | tf_op jit(solution)/shard_map/all_to_all | solution.py:145
  429.0 6.7 %all_gather.3 = f32[18,32,64]{1,2,0:T(8,128)S(1)} all-gather(f32[18,32,16]{1,2,0:T(8,128)S(1)} %copy.81), channel_id=1, replica_groups=mesh['gx'=8,'gy'=4] {'gy'}, dimensions={2}, use_global_device_ids=true | all-gather | bytes 184320 | tf_op jit(solution)/shard_map/all_gather | solution.py:146
  435.7 1.5 convolution_bitcast_fusion.2
  439.0 2.1 convolution_add_fusion
  (171 shorter events, 45.4 us)
Async XLA Ops:
  0.0 16.9 %copy-start.7 = (f32[3,3,21]{2,1,0:T(4,128)S(1)}, f32[3,3,21]{2,1,0:T(4,128)}, u32[]{:S(2)}) copy-start(f32[3,3,21]{2,1,0:T(4,128)} %param.9) | copy-start | bytes 2272
  2.9 42.7 %collective-permute-start = (f32[10,32,256]{2,0,1:T(8,128)}, f32[10,32,256]{2,0,1:T(8,128)}, u32[]{:S(2)}, u32[]{:S(2)}) collective-permute-start(f32[10,32,256]{2,0,1:T(8,128)} %get-tuple-element.10), channel_id=1, source_target_pairs={{0,4},{4,8},{8,12},{12,16},{16,20},{20,24},{24,28},{28,0},{1,5},{5... | collective-permute-start | bytes 983048 | tf_op jit(solution)/shard_map/ppermute | solution.py:16
  5.9 39.7 %collective-permute-start.1 = (f32[10,32,256]{2,0,1:T(8,128)}, f32[10,32,256]{2,0,1:T(8,128)}, u32[]{:S(2)}, u32[]{:S(2)}) collective-permute-start(f32[10,32,256]{2,0,1:T(8,128)} %get-tuple-element.11), channel_id=1, source_target_pairs={{4,0},{8,4},{12,8},{16,12},{20,16},{24,20},{28,24},{0,28},{5,1},{9... | collective-permute-start | bytes 983048 | tf_op jit(solution)/shard_map/ppermute | solution.py:17
  41.2 8.4 %copy-start.11 = (f32[3,128]{1,0:T(4,128)S(1)}, f32[3,128]{1,0:T(4,128)}, u32[]{:S(2)}) copy-start(f32[3,128]{1,0:T(4,128)} %convolution_bitcast_fusion.16) | copy-start | bytes 4612
  41.9 7.8 %copy-start.6 = (f32[3,256]{1,0:T(4,128)S(1)}, f32[3,256]{1,0:T(4,128)}, u32[]{:S(2)}) copy-start(f32[3,256]{1,0:T(4,128)} %convolution_bitcast_fusion.13) | copy-start | bytes 9220
  41.9 7.9 %copy-start.3 = (s32[16384]{0:T(1024)S(1)}, s32[16384]{0:T(1024)}, u32[]{:S(2)}) copy-start(s32[16384]{0:T(1024)} %fusion.83) | copy-start | bytes 196612
  44.1 340.4 %copy-start = (f32[3,18,38]{2,1,0:T(8,128)}, f32[3,18,38]{2,1,0:T(8,128)S(1)}, u32[]{:S(2)}) copy-start(f32[3,18,38]{2,1,0:T(8,128)S(1)} %bitcast_select_fusion.1) | copy-start | bytes 24628
  47.8 298.1 %collective-permute-start.2 = (f32[52,10,256]{2,0,1:T(8,128)}, f32[52,10,256]{2,0,1:T(8,128)}, u32[]{:S(2)}, u32[]{:S(2)}) collective-permute-start(f32[52,10,256]{2,0,1:T(8,128)} %get-tuple-element.6), channel_id=1, source_target_pairs={{0,1},{1,2},{2,3},{3,0},{4,5},{5,6},{6,7},{7,4},{8,9},{9,10},{10,1... | collective-permute-start | bytes 1597448 | tf_op jit(solution)/shard_map/ppermute | solution.py:16
  47.8 298.1 %collective-permute-start.3 = (f32[52,10,256]{2,0,1:T(8,128)S(1)}, f32[52,10,256]{2,0,1:T(8,128)}, u32[]{:S(2)}, u32[]{:S(2)}) collective-permute-start(f32[52,10,256]{2,0,1:T(8,128)S(1)} %get-tuple-element.8), channel_id=1, source_target_pairs={{1,0},{2,1},{3,2},{0,3},{5,4},{6,5},{7,6},{4,7},{9,8},{10,9},{11,1... | collective-permute-start | bytes 1597448 | tf_op jit(solution)/shard_map/ppermute | solution.py:17
  326.9 18.9 %copy-start.5 = (pred[128,128]{1,0:T(8,128)(4,1)S(1)}, pred[128,128]{1,0:T(8,128)(4,1)}, u32[]{:S(2)}) copy-start(pred[128,128]{1,0:T(8,128)(4,1)} %compare_and_fusion.1) | copy-start | bytes 49156
  326.9 18.9 %copy-start.2 = (pred[256,256]{1,0:T(8,128)(4,1)S(1)}, pred[256,256]{1,0:T(8,128)(4,1)}, u32[]{:S(2)}) copy-start(pred[256,256]{1,0:T(8,128)(4,1)} %compare_and_fusion) | copy-start | bytes 196612
  326.9 19.0 %copy-start.13 = (s32[52]{0:T(128)S(1)}, s32[52]{0:T(128)}, u32[]{:S(2)}) copy-start(s32[52]{0:T(128)} %iota_add_fusion.2) | copy-start | bytes 628
  326.9 19.0 %copy-start.14 = (s32[16]{0:T(128)S(1)}, s32[16]{0:T(128)}, u32[]{:S(2)}) copy-start(s32[16]{0:T(128)} %iota_multiply_fusion.4) | copy-start | bytes 196
  345.9 4.5 %copy-start.15 = (s32[128]{0:T(128)S(1)}, s32[128]{0:T(128)}, u32[]{:S(2)}) copy-start(s32[128]{0:T(128)} %iota_multiply_fusion.3) | copy-start | bytes 1540
  351.0 24.5 %collective-permute-start.4 = (f32[11,16,128]{2,1,0:T(8,128)S(1)}, f32[11,16,128]{2,1,0:T(8,128)S(1)}, u32[]{:S(2)}, u32[]{:S(2)}) collective-permute-start(f32[11,16,128]{2,1,0:T(8,128)S(1)} %get-tuple-element.17), channel_id=1, source_target_pairs={{0,4},{4,8},{8,12},{12,16},{16,20},{20,24},{24,28},{28,0},{1,5},{5... | collective-permute-start | bytes 270344 | tf_op jit(solution)/shard_map/ppermute | solution.py:16
  351.0 24.4 %collective-permute-start.5 = (f32[11,16,128]{2,1,0:T(8,128)S(1)}, f32[11,16,128]{2,1,0:T(8,128)S(1)}, u32[]{:S(2)}, u32[]{:S(2)}) collective-permute-start(f32[11,16,128]{2,1,0:T(8,128)S(1)} %get-tuple-element.18), channel_id=1, source_target_pairs={{4,0},{8,4},{12,8},{16,12},{20,16},{24,20},{28,24},{0,28},{5,1},{9... | collective-permute-start | bytes 270344 | tf_op jit(solution)/shard_map/ppermute | solution.py:17
  375.5 7.8 %collective-permute-start.6 = (f32[38,11,128]{2,1,0:T(8,128)S(1)}, f32[38,11,128]{2,1,0:T(8,128)S(1)}, u32[]{:S(2)}, u32[]{:S(2)}) collective-permute-start(f32[38,11,128]{2,1,0:T(8,128)S(1)} %get-tuple-element.15), channel_id=1, source_target_pairs={{0,1},{1,2},{2,3},{3,0},{4,5},{5,6},{6,7},{7,4},{8,9},{9,10},{10,1... | collective-permute-start | bytes 642056 | tf_op jit(solution)/shard_map/ppermute | solution.py:16
  375.6 8.8 %collective-permute-start.7 = (f32[38,11,128]{2,1,0:T(8,128)S(1)}, f32[38,11,128]{2,1,0:T(8,128)S(1)}, u32[]{:S(2)}, u32[]{:S(2)}) collective-permute-start(f32[38,11,128]{2,1,0:T(8,128)S(1)} %get-tuple-element.16), channel_id=1, source_target_pairs={{1,0},{2,1},{3,2},{0,3},{5,4},{6,5},{7,6},{4,7},{9,8},{10,9},{11,1... | collective-permute-start | bytes 642056 | tf_op jit(solution)/shard_map/ppermute | solution.py:17
  378.4 9.5 %copy-start.9 = (s32[38]{0:T(128)S(1)}, s32[38]{0:T(128)}, u32[]{:S(2)}) copy-start(s32[38]{0:T(128)} %iota_add_fusion.1) | copy-start | bytes 460
  378.4 9.5 %copy-start.10 = (s32[8]{0:T(128)S(1)}, s32[8]{0:T(128)}, u32[]{:S(2)}) copy-start(s32[8]{0:T(128)} %iota_multiply_fusion.1) | copy-start | bytes 100
  378.4 10.4 %copy-start.12 = (s32[64]{0:T(128)S(1)}, s32[64]{0:T(128)}, u32[]{:S(2)}) copy-start(s32[64]{0:T(128)} %iota_multiply_fusion.2) | copy-start | bytes 772
  385.1 4.5 %copy-start.1 = (f32[3,18,38]{2,1,0:T(8,128)S(1)}, f32[3,18,38]{2,1,0:T(8,128)}, u32[]{:S(2)}) copy-start(f32[3,18,38]{2,1,0:T(8,128)} %copy-done) | copy-start | bytes 24628
  390.0 11.1 %copy-start.4 = (f32[3,32,32]{2,1,0:T(8,128)S(1)}, f32[3,32,32]{2,1,0:T(8,128)}, u32[]{:S(2)}) copy-start(f32[3,32,32]{2,1,0:T(8,128)} %select_bitcast_fusion.3) | copy-start | bytes 36868
  391.8 7.3 %all-to-all-start = ((f32[4,1,3072]{2,1,0:T(1,128)}), f32[4,1,3072]{2,1,0:T(1,128)S(1)}, u32[]{:S(2)}, u32[]{:S(2)}) async-start(f32[4,1,3072]{2,1,0:T(1,128)} %reshape.394), calls=%async_computation | async-start | bytes 98304 | tf_op jit(solution)/shard_map/all_to_all | solution.py:130
  403.3 10.3 %all-to-all-start.1 = ((f32[8,1,1536]{2,1,0:T(1,128)}), f32[8,1,1536]{2,1,0:T(1,128)S(1)}, u32[]{:S(2)}, u32[]{:S(2)}) async-start(f32[8,1,1536]{2,1,0:T(1,128)} %reshape.396), calls=%async_computation.1 | async-start | bytes 98304 | tf_op jit(solution)/shard_map/all_to_all | solution.py:135
  416.7 21.0 %copy-start.8 = (s32[18]{0:T(128)S(1)}, s32[18]{0:T(128)}, u32[]{:S(2)}) copy-start(s32[18]{0:T(128)} %iota_multiply_fusion.5) | copy-start | bytes 220
  417.8 10.0 %all-to-all-start.2 = ((f32[8,1,1152]{2,1,0:T(1,128)}), f32[8,1,1152]{2,1,0:T(1,128)S(1)}, u32[]{:S(2)}, u32[]{:S(2)}) async-start(f32[8,1,1152]{2,1,0:T(1,128)} %reshape.398), calls=%async_computation.2 | async-start | bytes 73728 | tf_op jit(solution)/shard_map/all_to_all | solution.py:145
where the time goes:
time: 449 us; the launch traced here: 441 us
  local copies, waits for them, and re-layouts  328 us (73%)
  matrix products  41.7 us (9%)
  starting transfers between devices  25 us (6%)
  waiting for transfers between devices  21.9 us (5%)
  other arithmetic  16.7 us (4%)
  blocking collectives  6.68 us (1%)
    gather x8, local copies, waits for them, and re-layouts, cycle_taps(): return jnp.take(profile, (col_ids - row_ids) % length, axis=1)  311 us
    dot_general x35, matrix products, contract(): return jnp.einsum(formula, left, right, precision=lax.Precision.HIGHEST)  38.8 us
    ppermute x4, starting transfers between devices, padded_2(): after = lax.ppermute(first, axis, down)  11.7 us
  transfers between devices with their start and end apart: 11, of which 5 were waited for; matrix products, arithmetic and copies ran while one was open for 80% of the time, Pallas kernels for 0%

commit v1 on v0

--- a/solution.py
+++ b/solution.py
@@ -20,7 +20,7 @@
 
 
 def contract(formula, left, right):
-    return jnp.einsum(formula, left, right, precision=lax.Precision.HIGHEST)
+    return jnp.einsum(formula, left, right, precision=lax.Precision.HIGH)
 
 
 def grid_ids(count_rows, count_cols):
@@ -36,25 +36,26 @@
     return table
 
 
+def spread_taps(taps, offsets):
+    table = jnp.zeros((taps.shape[0],) + offsets.shape, jnp.float32)
+    for position in range(taps.shape[1]):
+        table = table + jnp.where(offsets == position, taps[:, position, None, None], 0.0)
+    return table
+
+
 def band_taps(taps, count_rows, count_cols):
     row_ids, col_ids = grid_ids(count_rows, count_cols)
-    offsets = col_ids - row_ids
-    tap_count = taps.shape[1]
-    inside = (offsets >= 0) & (offsets < tap_count)
-    picked = jnp.take(taps, jnp.clip(offsets, 0, tap_count - 1), axis=1)
-    return jnp.where(inside[None], picked, 0.0)
+    return spread_taps(taps, col_ids - row_ids)
 
 
 def cycle_taps(taps, length):
+    row_ids, col_ids = grid_ids(length, length)
     tap_count = taps.shape[1]
-    radius = tap_count // 2
-    wrapped = (jnp.arange(tap_count, dtype=jnp.int32) - radius) % length
-    onehot = (wrapped[:, None] == jnp.arange(length, dtype=jnp.int32)[None, :]).astype(jnp.float32)
-    profile = jnp.dot(
-        taps, onehot, preferred_element_type=jnp.float32, precision=lax.Precision.HIGHEST
-    )
-    row_ids, col_ids = grid_ids(length, length)
-    return jnp.take(profile, (col_ids - row_ids) % length, axis=1)
+    shift = (col_ids - row_ids + tap_count // 2) % length
+    table = spread_taps(taps, shift)
+    for lap in range(1, -(-tap_count // length)):
+        table = table + spread_taps(taps, shift + lap * length)
+    return table
 
 
 def restrict_band(count_rows, count_cols, margin):

time: 449 us -> 151 us (0.34); the launches traced: 441 us -> 150 us
  local copies, waits for them, and re-layouts: 328 us -> 13.9 us
  other arithmetic: 16.7 us -> 49 us
  matrix products: 41.7 us -> 24.4 us
  waiting for transfers between devices: 21.9 us -> 30.3 us
    gather x14 -> x0, local copies, waits for them, and re-layouts: 318 us -> none  [the longest x8 311 us: cycle_taps(): return jnp.take(profile, (col_ids - row_ids) % length, axis=1)]
    eq x0 -> x66, other arithmetic: none -> 32.9 us  [spread_taps(): offsets == position]
    dot_general x39 -> x35, matrix products: 40.8 us -> 23.6 us  [contract(): return jnp.einsum(formula, left, right, precision=lax.Precision.HIGH)]
    ppermute x4, waiting for transfers between devices: 4.9 us -> 14.2 us  [padded_2(): before = lax.ppermute(last, axis, up)]
    add x0 -> x6, other arithmetic: none -> 8.6 us  [spread_taps(): table + jnp.where(offsets == position, taps[:, position, None, None], 0.0)]
    slice x0 -> x5, local copies, waits for them, and re-layouts: none -> 4.65 us  [spread_taps(): taps[:, position, None, None]]
  transfers between devices with their start and end apart: 11 -> 11, of which waited for: 5 -> 7; matrix products, arithmetic and copies ran while one was open for 80% -> 42% of each run, Pallas kernels for 0% -> 0%
where the time goes in v1:
time: 151 us; the launch traced here: 150 us
  other arithmetic  49 us (32%)
  waiting for transfers between devices  30.3 us (20%)
  starting transfers between devices  24.5 us (16%)
  matrix products  24.4 us (16%)
  local copies, waits for them, and re-layouts  13.9 us (9%)
  blocking collectives  6.68 us (4%)
    eq x66, other arithmetic, spread_taps(): offsets == position  32.9 us
    dot_general x35, matrix products, contract(): return jnp.einsum(formula, left, right, precision=lax.Precision.HIGH)  23.6 us
    ppermute x4, waiting for transfers between devices, padded_2(): before = lax.ppermute(last, axis, up)  14.2 us
    ppermute x4, starting transfers between devices, padded_2(): after = lax.ppermute(first, axis, down)  11.1 us
    add x6, other arithmetic, spread_taps(): table + jnp.where(offsets == position, taps[:, position, None, None], 0.0)  8.6 us
    all_gather x1, blocking collectives, body(): returned = lax.all_gather(back_rows, 'gy', axis=2, tiled=True)  6.68 us
    all_to_all x1, waiting for transfers between devices, body(): lax.all_to_all(windows, 'gx', split_axis=0, concat_axis=2, tiled=True)[0]  6.39 us
    all_to_all x1, waiting for transfers between devices, body(): lax.all_to_all(turned_yz, 'gx', split_axis=2, concat_axis=1, tiled=True)  5.75 us
  transfers between devices with their start and end apart: 11, of which 7 were waited for; matrix products, arithmetic and copies ran while one was open for 42% of the time, Pallas kernels for 0%

profile of v1, /device:TPU:0, one launch (start us, length us, event | category | flops | bytes accessed | tf_op | source)
XLA Modules:
  0.0 150.2 jit_solution(10309947405876358656)
XLA Ops:
  0.0 1.8 %copy.17 = f32[32,32,256]{2,0,1:T(8,128)S(1)} copy(f32[32,32,256]{2,1,0:T(8,128)} %param.2) | data formatting | bytes 2097152 | tf_op args[0]
  1.9 3.0 %collective-permute-start = (f32[10,32,256]{2,0,1:T(8,128)S(1)}, f32[10,32,256]{2,0,1:T(8,128)S(1)}, u32[]{:S(2)}, u32[]{:S(2)}) collective-permute-start(f32[10,32,256]{2,0,1:T(8,128)S(1)} %get-tuple-element.70), channel_id=1, source_target_pairs={{0,4},{4,8},{8,12},{12,16},{16,20},{20,24},{24,28},{28,0},{1,5},{5... | collective-permute-start | bytes 983048 | tf_op jit(solution)/shard_map/ppermute | solution.py:16
  5.0 3.1 %collective-permute-start.1 = (f32[10,32,256]{2,0,1:T(8,128)S(1)}, f32[10,32,256]{2,0,1:T(8,128)S(1)}, u32[]{:S(2)}, u32[]{:S(2)}) collective-permute-start(f32[10,32,256]{2,0,1:T(8,128)S(1)} %get-tuple-element.71), channel_id=1, source_target_pairs={{4,0},{8,4},{12,8},{16,12},{20,16},{24,20},{28,24},{0,28},{5,1},{9... | collective-permute-start | bytes 983048 | tf_op jit(solution)/shard_map/ppermute | solution.py:17
  17.9 1.0 slice_reduce_fusion.41
  32.2 1.0 slice_reduce_fusion.62
  50.6 1.7 %select_add_fusion.3 = f32[3,32,32]{2,1,0:T(8,128)} fusion(f32[3]{0:T(128)} %get-tuple-element.6, f32[3]{0:T(128)} %get-tuple-element.7, f32[3]{0:T(128)} %get-tuple-element.8, f32[3]{0:T(128)} %get-tuple-element.9, f32[3]{0:T(128)} %get-tuple-element.10, f32[3]{0:T(128)} %get-tuple-element.11, f32[3]{0:T(128)} %get-tuple-element.12, ...), kind=kLoop, calls=%fused_computation.168 | loop fusion | flops 125952 | bytes 34044 | tf_op jit(solution)/shard_map/add | solution.py:42
  52.3 1.1 select_add_fusion.5
  53.4 1.1 select_add_fusion.4
  54.5 1.6 %select_add_fusion.1 = f32[3,128,128]{2,1,0:T(8,128)S(1)} fusion(f32[3]{0:T(128)} %get-tuple-element.27, f32[3]{0:T(128)} %get-tuple-element.28, f32[3]{0:T(128)} %get-tuple-element.29, f32[3]{0:T(128)} %get-tuple-element.30, f32[3]{0:T(128)} %get-tuple-element.31, f32[3]{0:T(128)} %get-tuple-element.32, f32[3]{0:T(128)} %get-tuple-element.33, ...), kind=kLoop, calls=%fused_computation.63 | loop fusion | flops 2015232 | bytes 540924 | tf_op jit(solution)/shard_map/add | solution.py:42
  56.7 1.7 %collective-permute-start.3 = (f32[52,10,256]{2,0,1:T(8,128)S(1)}, f32[52,10,256]{2,0,1:T(8,128)S(1)}, u32[]{:S(2)}, u32[]{:S(2)}) collective-permute-start(f32[52,10,256]{2,0,1:T(8,128)S(1)} %get-tuple-element.69), channel_id=1, source_target_pairs={{1,0},{2,1},{3,2},{0,3},{5,4},{6,5},{7,6},{4,7},{9,8},{10,9},{11,1... | collective-permute-start | bytes 1597448 | tf_op jit(solution)/shard_map/ppermute | solution.py:17
  58.8 2.2 %select_add_fusion = f32[3,256,256]{2,1,0:T(8,128)S(1)} fusion(f32[3]{0:T(128)S(1)} %copy-done.24, f32[3]{0:T(128)S(1)} %copy-done.25, f32[3]{0:T(128)S(1)} %copy-done.26, f32[3]{0:T(128)S(1)} %copy-done.27, f32[3]{0:T(128)S(1)} %copy-done.28, f32[3]{0:T(128)S(1)} %copy-done.29, f32[3]{0:T(128)S(1)} %copy-done.30, f32[3]{0:T(128)S(1)} %copy-done.31, ...), kind=kLoop, calls=%fused_computation.30 | loop fusion | flops 8060928 | bytes 2162940 | tf_op jit(solution)/shard_map/add | solution.py:42
  61.0 9.0 %collective-permute-done.2 = f32[52,10,256]{2,0,1:T(8,128)S(1)} collective-permute-done((f32[52,10,256]{2,0,1:T(8,128)S(1)}, f32[52,10,256]{2,0,1:T(8,128)S(1)}, u32[]{:S(2)}, u32[]{:S(2)}) %collective-permute-start.2) | collective-permute-done | bytes 532512 | tf_op jit(solution)/shard_map/ppermute | solution.py:16
  71.0 1.7 %fusion.222 = f32[16,52,256]{2,0,1:T(8,128)S(1)} fusion(s32[16]{0:T(128)} %iota_multiply_fusion.4, s32[52]{0:T(128)} %iota_add_fusion.2, f32[52,10,256]{2,0,1:T(8,128)S(1)} %collective-permute-done.3, f32[10,32,256]{2,0,1:T(8,128)S(1)} %collective-permute-done.1, f32[32,32,256]{2,0,1:T(8,128)S(1)} %copy.17, f32[10,32,256]{2,0,1:T(8,128)S(1)} %collective-permute-done, ...), kind=kOutput, calls=%fused_computation.369 | convolution fusion | flops 69235712 | bytes 3621136 | tf_op jit(solution)/shard_map/mc,cyz->myz/dot_general | solution.py:23
  74.1 4.7 %collective-permute-start.5 = (f32[11,16,128]{2,1,0:T(8,128)S(1)}, f32[11,16,128]{2,1,0:T(8,128)S(1)}, u32[]{:S(2)}, u32[]{:S(2)}) collective-permute-start(f32[11,16,128]{2,1,0:T(8,128)S(1)} %get-tuple-element.78), channel_id=1, source_target_pairs={{4,0},{8,4},{12,8},{16,12},{20,16},{24,20},{28,24},{0,28},{5,1},{9... | collective-permute-start | bytes 270344 | tf_op jit(solution)/shard_map/ppermute | solution.py:17
  78.8 1.0 fusion.172
  79.8 1.6 %fusion.9 = f32[32,32,256]{2,1,0:T(8,128)S(1)} fusion(f32[32,52,256]{2,0,1:T(8,128)S(1)} %fusion.172, f32[3,32,52]{2,1,0:T(8,128)S(1)} %select_add_fusion.4), kind=kOutput, calls=%fused_computation.8 | convolution fusion | flops 81788928 | bytes 2768896 | tf_op jit(solution)/shard_map/nc,mcz->mnz/dot_general | solution.py:23
  81.5 1.0 fusion.171
  82.5 1.6 %fusion.6 = f32[32,32,256]{2,1,0:T(8,128)S(1)} fusion(f32[32,52,256]{2,0,1:T(8,128)S(1)} %fusion.171, f32[3,32,52]{2,1,0:T(8,128)S(1)} %select_add_fusion.4), kind=kOutput, calls=%fused_computation.7 | convolution fusion | flops 81788928 | bytes 2768896 | tf_op jit(solution)/shard_map/nc,mcz->mnz/dot_general | solution.py:23
  85.4 1.0 fusion.173
  86.4 1.6 %fusion.12 = f32[32,32,256]{2,1,0:T(8,128)S(1)} fusion(f32[32,52,256]{2,0,1:T(8,128)S(1)} %fusion.173, f32[3,32,52]{2,1,0:T(8,128)S(1)} %select_add_fusion.4), kind=kOutput, calls=%fused_computation.9 | convolution fusion | flops 81788928 | bytes 2768896 | tf_op jit(solution)/shard_map/nc,mcz->mnz/dot_general | solution.py:23
  88.3 1.6 %collective-permute-start.7 = (f32[38,11,128]{2,1,0:T(8,128)S(1)}, f32[38,11,128]{2,1,0:T(8,128)S(1)}, u32[]{:S(2)}, u32[]{:S(2)}) collective-permute-start(f32[38,11,128]{2,1,0:T(8,128)S(1)} %get-tuple-element.76), channel_id=1, source_target_pairs={{1,0},{2,1},{3,2},{0,3},{5,4},{6,5},{7,6},{4,7},{9,8},{10,9},{11,1... | collective-permute-start | bytes 642056 | tf_op jit(solution)/shard_map/ppermute | solution.py:17
  90.6 5.1 %collective-permute-done.6 = f32[38,11,128]{2,1,0:T(8,128)S(1)} collective-permute-done((f32[38,11,128]{2,1,0:T(8,128)S(1)}, f32[38,11,128]{2,1,0:T(8,128)S(1)}, u32[]{:S(2)}, u32[]{:S(2)}) %collective-permute-start.6) | collective-permute-done | bytes 214048 | tf_op jit(solution)/shard_map/ppermute | solution.py:16
  95.7 1.4 collective-permute-done.7
  100.6 1.2 copy.32
  102.8 3.3 %all-to-all-start = ((f32[4,1,3072]{2,1,0:T(1,128)}), f32[4,1,3072]{2,1,0:T(1,128)S(1)}, u32[]{:S(2)}, u32[]{:S(2)}) async-start(f32[4,1,3072]{2,1,0:T(1,128)} %reshape.185), calls=%async_computation | async-start | bytes 98304 | tf_op jit(solution)/shard_map/all_to_all | solution.py:131
  108.6 1.5 all-to-all-done
  114.1 3.3 %all-to-all-start.1 = ((f32[8,1,1536]{2,1,0:T(1,128)}), f32[8,1,1536]{2,1,0:T(1,128)S(1)}, u32[]{:S(2)}, u32[]{:S(2)}) async-start(f32[8,1,1536]{2,1,0:T(1,128)} %reshape.187), calls=%async_computation.1 | async-start | bytes 98304 | tf_op jit(solution)/shard_map/all_to_all | solution.py:136
  118.5 5.7 %all-to-all-done.1 = f32[8,1,1536]{2,1,0:T(1,128)S(1)} async-done(((f32[8,1,1536]{2,1,0:T(1,128)}), f32[8,1,1536]{2,1,0:T(1,128)S(1)}, u32[]{:S(2)}, u32[]{:S(2)}) %all-to-all-start.1) | async-done | bytes 49184 | tf_op jit(solution)/shard_map/all_to_all | solution.py:136
  128.5 3.3 %all-to-all-start.2 = ((f32[8,1,1152]{2,1,0:T(1,128)}), f32[8,1,1152]{2,1,0:T(1,128)S(1)}, u32[]{:S(2)}, u32[]{:S(2)}) async-start(f32[8,1,1152]{2,1,0:T(1,128)} %reshape.189), calls=%async_computation.2 | async-start | bytes 73728 | tf_op jit(solution)/shard_map/all_to_all | solution.py:146
  132.1 6.4 %all-to-all-done.2 = f32[8,1,1152]{2,1,0:T(1,128)S(1)} async-done(((f32[8,1,1152]{2,1,0:T(1,128)}), f32[8,1,1152]{2,1,0:T(1,128)S(1)}, u32[]{:S(2)}, u32[]{:S(2)}) %all-to-all-start.2) | async-done | bytes 36896 | tf_op jit(solution)/shard_map/all_to_all | solution.py:146
  139.7 6.7 %all_gather.3 = f32[18,32,64]{1,2,0:T(8,128)S(1)} all-gather(f32[18,32,16]{1,2,0:T(8,128)S(1)} %copy.48), channel_id=1, replica_groups=mesh['gx'=8,'gy'=4] {'gy'}, dimensions={2}, use_global_device_ids=true | all-gather | bytes 184320 | tf_op jit(solution)/shard_map/all_gather | solution.py:147
  148.5 1.7 %convolution_add_fusion = f32[32,32,256]{2,1,0:T(8,128)} fusion(f32[32,32,256]{2,1,0:T(8,128)S(1)} %convolution_add_fusion.1, f32[32,32,128]{2,1,0:T(8,128)S(1)} %convolution_bitcast_fusion, s32[128]{0:T(128)S(1)} %copy-done.49), kind=kOutput, calls=%fused_computation.10 | convolution fusion | flops 202473472 | bytes 2621952 | tf_op jit(solution)/shard_map/mjz,wz->mjw/dot_general | solution.py:23
  (261 shorter events, 64.6 us)
Async XLA Ops:
  1.8 14.3 %copy-start.22 = (f32[3,3,21]{2,1,0:T(4,128)S(1)}, f32[3,3,21]{2,1,0:T(4,128)}, u32[]{:S(2)}) copy-start(f32[3,3,21]{2,1,0:T(4,128)} %param.3) | copy-start | bytes 2272
  1.9 54.5 %collective-permute-start = (f32[10,32,256]{2,0,1:T(8,128)S(1)}, f32[10,32,256]{2,0,1:T(8,128)S(1)}, u32[]{:S(2)}, u32[]{:S(2)}) collective-permute-start(f32[10,32,256]{2,0,1:T(8,128)S(1)} %get-tuple-element.70), channel_id=1, source_target_pairs={{0,4},{4,8},{8,12},{12,16},{16,20},{20,24},{24,28},{28,0},{1,5},{5... | collective-permute-start | bytes 983048 | tf_op jit(solution)/shard_map/ppermute | solution.py:16
  5.0 51.5 %collective-permute-start.1 = (f32[10,32,256]{2,0,1:T(8,128)S(1)}, f32[10,32,256]{2,0,1:T(8,128)S(1)}, u32[]{:S(2)}, u32[]{:S(2)}) collective-permute-start(f32[10,32,256]{2,0,1:T(8,128)S(1)} %get-tuple-element.71), channel_id=1, source_target_pairs={{4,0},{8,4},{12,8},{16,12},{20,16},{24,20},{28,24},{0,28},{5,1},{9... | collective-permute-start | bytes 983048 | tf_op jit(solution)/shard_map/ppermute | solution.py:17
  53.4 46.2 %copy-start = (f32[3,18,38]{2,1,0:T(8,128)}, f32[3,18,38]{2,1,0:T(8,128)S(1)}, u32[]{:S(2)}) copy-start(f32[3,18,38]{2,1,0:T(8,128)S(1)} %select_add_fusion.5) | copy-start | bytes 24628
  56.0 2.4 %copy-start.1 = (pred[256,256]{1,0:T(8,128)(4,1)S(1)}, pred[256,256]{1,0:T(8,128)(4,1)}, u32[]{:S(2)}) copy-start(pred[256,256]{1,0:T(8,128)(4,1)} %get-tuple-element.149) | copy-start | bytes 196612
  56.1 2.4 %copy-start.2 = (pred[256,256]{1,0:T(8,128)(4,1)S(1)}, pred[256,256]{1,0:T(8,128)(4,1)}, u32[]{:S(2)}) copy-start(pred[256,256]{1,0:T(8,128)(4,1)} %get-tuple-element.150) | copy-start | bytes 196612
  56.1 2.3 %copy-start.3 = (pred[256,256]{1,0:T(8,128)(4,1)S(1)}, pred[256,256]{1,0:T(8,128)(4,1)}, u32[]{:S(2)}) copy-start(pred[256,256]{1,0:T(8,128)(4,1)} %get-tuple-element.151) | copy-start | bytes 196612
  56.1 2.3 %copy-start.4 = (pred[256,256]{1,0:T(8,128)(4,1)S(1)}, pred[256,256]{1,0:T(8,128)(4,1)}, u32[]{:S(2)}) copy-start(pred[256,256]{1,0:T(8,128)(4,1)} %get-tuple-element.152) | copy-start | bytes 196612
  56.1 2.3 %copy-start.5 = (pred[256,256]{1,0:T(8,128)(4,1)S(1)}, pred[256,256]{1,0:T(8,128)(4,1)}, u32[]{:S(2)}) copy-start(pred[256,256]{1,0:T(8,128)(4,1)} %get-tuple-element.153) | copy-start | bytes 196612
  56.1 2.3 %copy-start.6 = (pred[256,256]{1,0:T(8,128)(4,1)S(1)}, pred[256,256]{1,0:T(8,128)(4,1)}, u32[]{:S(2)}) copy-start(pred[256,256]{1,0:T(8,128)(4,1)} %get-tuple-element.154) | copy-start | bytes 196612
  56.1 2.3 %copy-start.7 = (pred[256,256]{1,0:T(8,128)(4,1)S(1)}, pred[256,256]{1,0:T(8,128)(4,1)}, u32[]{:S(2)}) copy-start(pred[256,256]{1,0:T(8,128)(4,1)} %get-tuple-element.155) | copy-start | bytes 196612
  56.1 2.3 %copy-start.8 = (pred[256,256]{1,0:T(8,128)(4,1)S(1)}, pred[256,256]{1,0:T(8,128)(4,1)}, u32[]{:S(2)}) copy-start(pred[256,256]{1,0:T(8,128)(4,1)} %get-tuple-element.156) | copy-start | bytes 196612
  56.1 2.3 %copy-start.9 = (pred[256,256]{1,0:T(8,128)(4,1)S(1)}, pred[256,256]{1,0:T(8,128)(4,1)}, u32[]{:S(2)}) copy-start(pred[256,256]{1,0:T(8,128)(4,1)} %get-tuple-element.157) | copy-start | bytes 196612
  56.1 2.3 %copy-start.10 = (pred[256,256]{1,0:T(8,128)(4,1)S(1)}, pred[256,256]{1,0:T(8,128)(4,1)}, u32[]{:S(2)}) copy-start(pred[256,256]{1,0:T(8,128)(4,1)} %get-tuple-element.158) | copy-start | bytes 196612
  56.2 2.3 %copy-start.11 = (pred[256,256]{1,0:T(8,128)(4,1)S(1)}, pred[256,256]{1,0:T(8,128)(4,1)}, u32[]{:S(2)}) copy-start(pred[256,256]{1,0:T(8,128)(4,1)} %get-tuple-element.159) | copy-start | bytes 196612
  56.6 13.4 %collective-permute-start.2 = (f32[52,10,256]{2,0,1:T(8,128)S(1)}, f32[52,10,256]{2,0,1:T(8,128)S(1)}, u32[]{:S(2)}, u32[]{:S(2)}) collective-permute-start(f32[52,10,256]{2,0,1:T(8,128)S(1)} %get-tuple-element.68), channel_id=1, source_target_pairs={{0,1},{1,2},{2,3},{3,0},{4,5},{5,6},{6,7},{7,4},{8,9},{9,10},{10,1... | collective-permute-start | bytes 1597448 | tf_op jit(solution)/shard_map/ppermute | solution.py:16
  56.7 14.4 %collective-permute-start.3 = (f32[52,10,256]{2,0,1:T(8,128)S(1)}, f32[52,10,256]{2,0,1:T(8,128)S(1)}, u32[]{:S(2)}, u32[]{:S(2)}) collective-permute-start(f32[52,10,256]{2,0,1:T(8,128)S(1)} %get-tuple-element.69), channel_id=1, source_target_pairs={{1,0},{2,1},{3,2},{0,3},{5,4},{6,5},{7,6},{4,7},{9,8},{10,9},{11,1... | collective-permute-start | bytes 1597448 | tf_op jit(solution)/shard_map/ppermute | solution.py:17
  70.0 2.7 %copy-start.47 = (s32[52]{0:T(128)S(1)}, s32[52]{0:T(128)}, u32[]{:S(2)}) copy-start(s32[52]{0:T(128)} %iota_add_fusion.2) | copy-start | bytes 628
  70.0 2.7 %copy-start.48 = (s32[16]{0:T(128)S(1)}, s32[16]{0:T(128)}, u32[]{:S(2)}) copy-start(s32[16]{0:T(128)} %iota_multiply_fusion.4) | copy-start | bytes 196
  70.1 3.5 %copy-start.49 = (s32[128]{0:T(128)S(1)}, s32[128]{0:T(128)}, u32[]{:S(2)}) copy-start(s32[128]{0:T(128)} %iota_multiply_fusion.3) | copy-start | bytes 1540
  74.0 14.0 %collective-permute-start.4 = (f32[11,16,128]{2,1,0:T(8,128)S(1)}, f32[11,16,128]{2,1,0:T(8,128)S(1)}, u32[]{:S(2)}, u32[]{:S(2)}) collective-permute-start(f32[11,16,128]{2,1,0:T(8,128)S(1)} %get-tuple-element.77), channel_id=1, source_target_pairs={{0,4},{4,8},{8,12},{12,16},{16,20},{20,24},{24,28},{28,0},{1,5},{5... | collective-permute-start | bytes 270344 | tf_op jit(solution)/shard_map/ppermute | solution.py:16
  74.1 14.0 %collective-permute-start.5 = (f32[11,16,128]{2,1,0:T(8,128)S(1)}, f32[11,16,128]{2,1,0:T(8,128)S(1)}, u32[]{:S(2)}, u32[]{:S(2)}) collective-permute-start(f32[11,16,128]{2,1,0:T(8,128)S(1)} %get-tuple-element.78), channel_id=1, source_target_pairs={{4,0},{8,4},{12,8},{16,12},{20,16},{24,20},{28,24},{0,28},{5,1},{9... | collective-permute-start | bytes 270344 | tf_op jit(solution)/shard_map/ppermute | solution.py:17
  88.1 7.6 %collective-permute-start.6 = (f32[38,11,128]{2,1,0:T(8,128)S(1)}, f32[38,11,128]{2,1,0:T(8,128)S(1)}, u32[]{:S(2)}, u32[]{:S(2)}) collective-permute-start(f32[38,11,128]{2,1,0:T(8,128)S(1)} %get-tuple-element.75), channel_id=1, source_target_pairs={{0,1},{1,2},{2,3},{3,0},{4,5},{5,6},{6,7},{7,4},{8,9},{9,10},{10,1... | collective-permute-start | bytes 642056 | tf_op jit(solution)/shard_map/ppermute | solution.py:16
  88.3 8.8 %collective-permute-start.7 = (f32[38,11,128]{2,1,0:T(8,128)S(1)}, f32[38,11,128]{2,1,0:T(8,128)S(1)}, u32[]{:S(2)}, u32[]{:S(2)}) collective-permute-start(f32[38,11,128]{2,1,0:T(8,128)S(1)} %get-tuple-element.76), channel_id=1, source_target_pairs={{1,0},{2,1},{3,2},{0,3},{5,4},{6,5},{7,6},{4,7},{9,8},{10,9},{11,1... | collective-permute-start | bytes 642056 | tf_op jit(solution)/shard_map/ppermute | solution.py:17
  90.6 6.7 %copy-start.43 = (s32[38]{0:T(128)S(1)}, s32[38]{0:T(128)}, u32[]{:S(2)}) copy-start(s32[38]{0:T(128)} %iota_add_fusion.1) | copy-start | bytes 460
  90.6 6.7 %copy-start.44 = (s32[8]{0:T(128)S(1)}, s32[8]{0:T(128)}, u32[]{:S(2)}) copy-start(s32[8]{0:T(128)} %iota_multiply_fusion.1) | copy-start | bytes 100
  90.6 7.3 %copy-start.45 = (s32[64]{0:T(128)S(1)}, s32[64]{0:T(128)}, u32[]{:S(2)}) copy-start(s32[64]{0:T(128)} %iota_multiply_fusion.2) | copy-start | bytes 772
  102.8 7.3 %all-to-all-start = ((f32[4,1,3072]{2,1,0:T(1,128)}), f32[4,1,3072]{2,1,0:T(1,128)S(1)}, u32[]{:S(2)}, u32[]{:S(2)}) async-start(f32[4,1,3072]{2,1,0:T(1,128)} %reshape.185), calls=%async_computation | async-start | bytes 98304 | tf_op jit(solution)/shard_map/all_to_all | solution.py:131
  108.1 4.2 %copy-start.21 = (f32[3,32,32]{2,1,0:T(8,128)S(1)}, f32[3,32,32]{2,1,0:T(8,128)}, u32[]{:S(2)}) copy-start(f32[3,32,32]{2,1,0:T(8,128)} %select_add_fusion.3) | copy-start | bytes 36868
  114.1 10.1 %all-to-all-start.1 = ((f32[8,1,1536]{2,1,0:T(1,128)}), f32[8,1,1536]{2,1,0:T(1,128)S(1)}, u32[]{:S(2)}, u32[]{:S(2)}) async-start(f32[8,1,1536]{2,1,0:T(1,128)} %reshape.187), calls=%async_computation.1 | async-start | bytes 98304 | tf_op jit(solution)/shard_map/all_to_all | solution.py:136
  127.4 18.9 %copy-start.46 = (s32[32]{0:T(128)S(1)}, s32[32]{0:T(128)}, u32[]{:S(2)}) copy-start(s32[32]{0:T(128)} %iota_multiply_fusion) | copy-start | bytes 388
  128.5 10.0 %all-to-all-start.2 = ((f32[8,1,1152]{2,1,0:T(1,128)}), f32[8,1,1152]{2,1,0:T(1,128)S(1)}, u32[]{:S(2)}, u32[]{:S(2)}) async-start(f32[8,1,1152]{2,1,0:T(1,128)} %reshape.189), calls=%async_computation.2 | async-start | bytes 73728 | tf_op jit(solution)/shard_map/all_to_all | solution.py:146
  (29 other events, 68.0 us)

commit v2 on v1

v2 whole, which is shorter than its diff:
```python
import functools

import jax
import jax.numpy as jnp
import numpy as np
from jax import lax
from jax.experimental import pallas as pl
from jax.experimental.pallas import tpu as pltpu
from jax.sharding import PartitionSpec as P

SPLINE = (0.125, 0.5, 0.75, 0.5, 0.125)
F32, BF16 = jnp.float32, jnp.bfloat16
MESH = pl.DeviceIdType.MESH


def spline_at(offset):
    return SPLINE[offset + 2] if -2 <= offset <= 2 else 0.0


def fixed_table(rows, cols, width):
    table = np.zeros((width, len(cols)), np.float32)
    for a, fine in enumerate(rows):
        for b, other in enumerate(cols):
            if fine is not None and other is not None:
                table[a, b] = spline_at(other - 2 * fine)
    return table


def lifted_table(rows, cols, width):
    table = np.zeros((width, len(cols)), np.float32)
    for a, fine in enumerate(rows):
        for b, coarse in enumerate(cols):
            if coarse is not None:
                table[a, b] = spline_at(fine - 2 * coarse)
    return table


def twice(table):
    return jnp.asarray(np.concatenate([table, table], axis=1), BF16)


def halves(value):
    high = value.astype(BF16)
    return high, (value - high.astype(F32)).astype(BF16)


def dot(left, right):
    return jnp.dot(left, right, preferred_element_type=F32)


def stacked2(value):
    high, low = halves(value)
    return jnp.concatenate([high, low], axis=0)


def stacked3(value):
    high, low = halves(value)
    return jnp.concatenate([high, low, high], axis=0)


def repeat(count, step, body):
    def trip(i, carry):
        for k in range(step):
            body(i * step + k)
        return carry

    assert count % step == 0
    lax.fori_loop(0, count // step, trip, 0)


def kernel(nx, ny, radius, terms, taps, q, ry1, rz1, ry2, rz2, uy2, uz2, uy1, uz1, out,
           fine, mid, own2, line2, top, ty0, ty1, ty2, tz0, tz1, tz2,
           y0, s0, y1, s1, y2, s2, rx, r1, l1w, l2x, l2y, tx, ty, md, mx, my,
           send, recv):
    bx, by, bz = q.shape
    hx, hy, hz = bx // 2, by // 2, bz // 2
    ex, ey, ez = bx // 4, by // 4, bz // 4
    count = 2 * radius + 1
    margin = radius + 1
    me_x, me_y = lax.axis_index("gx"), lax.axis_index("gy")
    reach = 2
    wy = min(ny, 2 * reach + 1)
    low_y = -((wy - 1) // 2)

    def device(dx, dy):
        return {"gx": lax.rem(me_x + dx + nx, nx), "gy": lax.rem(me_y + dy + ny, ny)}

    peers = {}
    for dx, dy in [(a, b) for a in (-1, 0, 1) for b in (-1, 0, 1)] + [(-2, 0), (2, 0)] + [
        (0, -(low_y + k)) for k in range(wy)
    ]:
        if dx % nx or dy % ny:
            peers[(dx % nx, dy % ny)] = (dx, dy)
    barrier = pltpu.get_barrier_semaphore()
    for dx, dy in peers.values():
        pl.semaphore_signal(barrier, inc=1, device_id=device(dx, dy), device_id_type=MESH)

    def tap(level, member, position):
        return taps[(level * terms + member) * count + position]

    def band(level, member, rows, cols, first, cycle):
        offsets = (
            lax.broadcasted_iota(jnp.int32, (rows, cols), 1)
            - lax.broadcasted_iota(jnp.int32, (rows, cols), 0)
            + first
        )
        if cycle:
            offsets = jnp.where(offsets < 0, offsets + cycle, offsets)
            offsets = jnp.where(offsets >= cycle, offsets - cycle, offsets)
        table = jnp.zeros((rows, cols), F32)
        for position in range(count):
            table = jnp.where(offsets == position, tap(level, member, position), table)
        return table

    def y_table(ref, level, rows, cols, first, cycle):
        for member in range(terms):
            high, low = halves(band(level, member, rows, cols, first, cycle))
            at = slice(member * rows, (member + 1) * rows)
            ref[at, 0:cols] = high
            ref[at, cols : 2 * cols] = high
            ref[at, 2 * cols : 3 * cols] = low

    def z_table(ref, level, n):
        def rows_of(i):
            start = pl.multiple_of(i * 16, 16)
            offsets = (
                lax.broadcasted_iota(jnp.int32, (16, n), 0)
                + start
                - lax.broadcasted_iota(jnp.int32, (16, n), 1)
                + radius
            )
            offsets = jnp.where(offsets < 0, offsets + n, offsets)
            offsets = jnp.where(offsets >= n, offsets - n, offsets)
            for member in range(terms):
                table = jnp.zeros((16, n), F32)
                for position in range(count):
                    table = jnp.where(offsets == position, tap(level, member, position), table)
                high, low = halves(table)
                ref[member, 0, pl.ds(start, 16), :] = high
                ref[member, 1, pl.ds(start, 16), :] = low

        repeat(n // 16, 1, rows_of)

    sem = [0]

    def remote(source, target, dx, dy):
        index = sem[0]
        sem[0] += 1
        return pltpu.make_async_remote_copy(
            src_ref=source, dst_ref=target, send_sem=send.at[index], recv_sem=recv.at[index],
            device_id=device(dx, dy), device_id_type=MESH,
        )

    def both(copies):
        for copy in copies:
            copy.start()
        return copies

    def arrive(copies):
        for copy in copies:
            copy.wait_recv()

    pad = 2 * 8
    x0, x1, c0, c1 = radius, radius + bx, pad, pad + by
    back, ahead = 6, 3

    fine[x0:x1, c0:c1, :] = q[...]
    y_table(ty0, 0, by, by + 2 * pad, radius - pad, 0)
    pl.semaphore_wait(barrier, len(peers))
    near = []
    for dx, src_x, dst_x in ((1, (bx - back, bx), (x0 - back, x0)), (-1, (0, ahead), (x1, x1 + ahead)), (0, (0, bx), (x0, x1))):
        for dy, src_y, dst_y in ((1, (by - 8, by), (c0 - 8, c0)), (-1, (0, 8), (c1, c1 + 8)), (0, (0, by), (c0, c1))):
            if dx or dy:
                near.append(remote(q.at[slice(*src_x), slice(*src_y)], fine.at[slice(*dst_x), slice(*dst_y)], dx, dy))
    both(near)
    far = [
        remote(q.at[bx - radius : bx - back], fine.at[0 : x0 - back, c0:c1], 1, 0),
        remote(q.at[ahead:radius], fine.at[x1 + ahead : x1 + radius, c0:c1], -1, 0),
        remote(q.at[:, by - 16 : by - 8], fine.at[x0:x1, 0:8], 0, 1),
        remote(q.at[:, 8:16], fine.at[x0:x1, c1 + 8 : c1 + 16], 0, -1),
    ]
    y_table(ty1, 1, ty1.shape[0] // terms, hy + 2 * hy, radius - 1 * hy - (-1) , 0)
    y_table(ty2, 2, ty2.shape[0] // terms, wy * ey, low_y * ey + 1 + radius, wy * ey if ny <= 2 * reach + 1 else 0)
    z_table(tz0, 0, bz)
    z_table(tz1, 1, hz)
    z_table(tz2, 2, ez)
    arrive(near)

    rows1 = hx + 3
    base = x0 - back

    def restrict_x(i):
        total = None
        for k in range(5):
            piece = fine[base + 2 * i + k, c0 - 8 : c1 + 8, :] * SPLINE[k]
            total = piece if total is None else total + piece
        r1[i] = dot(ry1[...], stacked2(total))

    repeat(rows1, 1 if rows1 % 19 else 19, restrict_x)
    wide1 = ry1.shape[0]
    high, low = halves(r1[...].reshape(rows1 * wide1, bz))
    l1w[...] = (dot(high, rz1[...]) + dot(low, rz1[...])).reshape(rows1, wide1, hz)
    m0, m1, d0, d1 = margin, margin + hx, hy, 2 * hy
    mid[m0:m1, d0:d1, :] = l1w[2 : 2 + hx, 0:hy, :]
    for i in range(ex):
        total = None
        for k in range(5):
            piece = l1w[2 * i + k] * SPLINE[k]
            total = piece if total is None else total + piece
        l2y[i] = dot(ry2[...], stacked2(total))
    high, low = halves(l2y[...].reshape(ex * ey, hz))
    line2[reach * ex : (reach + 1) * ex] = (dot(high, rz2[...]) + dot(low, rz2[...])).reshape(ex, ey, ez)

    home = line2.at[reach * ex : (reach + 1) * ex]
    lines = both([
        remote(home, line2.at[(reach - d) * ex : (reach - d + 1) * ex], d, 0) for d in (1, -1, 2, -2)
    ])
    rim = both([
        remote(mid.at[m1 - margin : m1, d0:d1], mid.at[0:m0, d0:d1], 1, 0),
        remote(mid.at[m0 : m0 + margin, d0:d1], mid.at[m1 : m1 + margin, d0:d1], -1, 0),
        remote(mid.at[m0:m1, d0:d1], mid.at[m0:m1, 0:d0], 0, 1),
        remote(mid.at[m0:m1, d0:d1], mid.at[m0:m1, d1 : d1 + hy], 0, -1),
    ])
    both(far)
    arrive(lines)
    spot = -low_y
    top[:, spot * ey : (spot + 1) * ey, :] = line2[...]
    fan = both([
        remote(line2, top.at[:, (k * ey) : (k + 1) * ey], 0, -(low_y + k)) for k in range(wy) if low_y + k
    ])
    arrive(rim[:2])
    rim += both([
        remote(mid.at[0:m0, d0:d1], mid.at[0:m0, 0:d0], 0, 1),
        remote(mid.at[m1 : m1 + margin, d0:d1], mid.at[m1 : m1 + margin, 0:d0], 0, 1),
        remote(mid.at[0:m0, d0:d1], mid.at[0:m0, d1 : d1 + hy], 0, -1),
        remote(mid.at[m1 : m1 + margin, d0:d1], mid.at[m1 : m1 + margin, d1 : d1 + hy], 0, -1),
    ])
    arrive(far[:2])
    wide = [(0, x0), (x1, x1 + radius)]
    slim = [(0, x0 - back), (x1 + ahead, x1 + radius)]
    corner = both(
        [remote(fine.at[a:b, c1 - 16 : c1 - 8], fine.at[a:b, 0:8], 0, 1) for a, b in wide]
        + [remote(fine.at[a:b, c1 - 8 : c1], fine.at[a:b, 8:16], 0, 1) for a, b in slim]
        + [remote(fine.at[a:b, c0 + 8 : c0 + 16], fine.at[a:b, c1 + 8 : c1 + 16], 0, -1) for a, b in wide]
        + [remote(fine.at[a:b, c0 : c0 + 8], fine.at[a:b, c1 : c1 + 8], 0, -1) for a, b in slim]
    )

    def correlate_y(ref, source, table, rows, step):
        width = table.shape[0] // terms

        def one(i):
            value = dot(table[...], stacked3(source[i]))
            for member in range(terms):
                ref[member, i] = value[member * width : (member + 1) * width]

        repeat(rows, step, one)

    def correlate_x(ref, source, level, rows, first, step):
        def one(i):
            for member in range(terms):
                total = None
                for position in range(count):
                    piece = source[member, i + first + position] * tap(level, member, position)
                    total = piece if total is None else total + piece
                high, low = halves(total)
                ref[member, 0, i] = high
                ref[member, 1, i] = low

        repeat(rows, step, one)

    def correlate_z(ref, table, a, b):
        size = (b - a) * ref.shape[3]
        total = None
        for member in range(terms):
            high = ref[member, 0, a:b].reshape(size, ref.shape[4])
            low = ref[member, 1, a:b].reshape(size, ref.shape[4])
            piece = dot(high, table[member, 0]) + dot(low, table[member, 0]) + dot(high, table[member, 1])
            total = piece if total is None else total + piece
        return total

    def prolong_x(source, j, first):
        at = j - 2 * first
        if j % 2 == 0:
            c = (j // 2) - first
            return source[c - 1] * 0.125 + source[c] * 0.75 + source[c + 1] * 0.125
        c = (j - 1) // 2 - first
        return source[c] * 0.5 + source[c + 1] * 0.5

    arrive(fan)
    correlate_y(y2, top, ty2, (2 * reach + 1) * ex, 8)
    rows2 = ex + 3
    correlate_x(s2, y2, 2, rows2, reach * ex - 1 - radius, 1)
    tx[...] = correlate_z(s2, tz2, 0, rows2).reshape(tx.shape)
    for j in range(hx + 2):
        ty[j] = dot(uy2[...], stacked2(prolong_x(tx, j - 1, -1)))
    high, low = halves(ty[...].reshape((hx + 2) * ty.shape[1], ez))
    lifted = dot(high, uz2[...]) + dot(low, uz2[...])

    md[...] = lifted.reshape(md.shape)
    arrive(rim[2:])
    correlate_y(y1, mid, ty1, hx + 2 * margin, 2)
    correlate_x(s1, y1, 1, hx + 2, 0, 1)
    md[...] += correlate_z(s1, tz1, 0, hx + 2).reshape(md.shape)
    for j in range(bx):
        high, low = halves(dot(uy1[...], stacked2(prolong_x(md, j, -1))))
        my[0, j] = high
        my[1, j] = low

    arrive(far[2:])
    arrive(corner)
    correlate_y(y0, fine, ty0, bx + 2 * radius, 4)
    correlate_x(s0, y0, 0, bx, 0, 1)
    for a in range(0, bx, 8):
        total = correlate_z(s0, tz0, a, a + 8)
        high = my[0, a : a + 8].reshape(8 * by, hz)
        low = my[1, a : a + 8].reshape(8 * by, hz)
        total = total + dot(high, uz1[...]) + dot(low, uz1[...])
        out[a : a + 8] = total.reshape(8, by, bz)
    for copy in near + far + lines + rim + fan + corner:
        copy.wait_send()


def cyclic_restrict(n):
    rows = np.arange(n)[:, None]
    cols = np.arange(n // 2)[None, :]
    table = np.zeros((n, n // 2), np.float32)
    for k in range(-2, 3):
        table += SPLINE[k + 2] * ((2 * cols + k) % n == rows)
    return table


def body(charges, kernel_taps):
    nx, ny = lax.axis_size("gx"), lax.axis_size("gy")
    levels, terms, count = kernel_taps.shape
    radius = count // 2
    margin = radius + 1
    bx, by, bz = charges.shape
    hx, hy, hz = bx // 2, by // 2, bz // 2
    ex, ey, ez = bx // 4, by // 4, bz // 4
    pad = 16
    wy = min(ny, 5)
    order1 = list(range(hy)) + [-2, -1, hy] + [None] * 5
    ry1 = fixed_table(order1, list(range(-8, by + 8)), len(order1))
    ry2 = fixed_table(list(range(ey)), order1, ey)
    rz1, rz2 = cyclic_restrict(bz), cyclic_restrict(hz)
    wide1 = hy + 8
    wide2 = ey + 8
    uy2 = lifted_table(list(range(-1, hy + 1)), list(range(-1, ey + 2)) + [None] * (wide2 - ey - 3), wide1)
    uy1 = lifted_table(list(range(by)), list(range(-1, hy + 1)) + [None] * (wide1 - hy - 2), by)
    fixed = [twice(ry1), jnp.asarray(rz1, BF16), twice(ry2), jnp.asarray(rz2, BF16), twice(uy2),
             jnp.asarray(rz2.T, BF16), twice(uy1), jnp.asarray(rz1.T, BF16)]
    rows1, rows2 = hx + 3, ex + 3
    vmem = lambda shape, dtype=F32: pltpu.VMEM(shape, dtype)
    scratch = [
        vmem((bx + 2 * radius, by + 2 * pad, bz)),
        vmem((hx + 2 * margin, 3 * hy, hz)),
        vmem((8, 128)),
        vmem((5 * ex, ey, ez)),
        vmem((5 * ex, wy * ey, ez)),
        vmem((terms * by, 3 * (by + 2 * pad)), BF16),
        vmem((terms * wide1, 9 * hy), BF16),
        vmem((terms * wide2, 3 * wy * ey), BF16),
        vmem((terms, 2, bz, bz), BF16),
        vmem((terms, 2, hz, hz), BF16),
        vmem((terms, 2, ez, ez), BF16),
        vmem((terms, bx + 2 * radius, by, bz)),
        vmem((terms, 2, bx, by, bz), BF16),
        vmem((terms, hx + 2 * margin, wide1, hz)),
        vmem((terms, 2, hx + 2, wide1, hz), BF16),
        vmem((terms, 5 * ex, wide2, ez)),
        vmem((terms, 2, rows2, wide2, ez), BF16),
        vmem((8, 128)),
        vmem((rows1, wide1, bz)),
        vmem((rows1, wide1, hz)),
        vmem((8, 128)),
        vmem((ex, ey, hz)),
        vmem((rows2, wide2, ez)),
        vmem((hx + 2, wide1, ez)),
        vmem((hx + 2, wide1, hz)),
        vmem((8, 128)),
        vmem((2, bx, by, hz), BF16),
        pltpu.SemaphoreType.DMA((48,)),
        pltpu.SemaphoreType.DMA((48,)),
    ]
    return pl.pallas_call(
        functools.partial(kernel, nx, ny, radius, terms),
        out_shape=jax.ShapeDtypeStruct(charges.shape, F32),
        in_specs=[pl.BlockSpec(memory_space=pltpu.SMEM)] + [pl.BlockSpec(memory_space=pltpu.VMEM)] * 9,
        out_specs=pl.BlockSpec(memory_space=pltpu.VMEM),
        scratch_shapes=scratch,
        compiler_params=pltpu.CompilerParams(
            collective_id=0, has_side_effects=True, vmem_limit_bytes=60 * 2**20
        ),
    )(kernel_taps.reshape(-1), charges, *fixed)


def solution(mesh):
    return jax.shard_map(
        body,
        mesh=mesh,
        in_specs=(P("gx", "gy", None), P()),
        out_specs=P("gx", "gy", None),
        check_vma=False,
    )
```

time: 151 us -> 61.5 us (0.41)
  Pallas kernels: 0 us -> 56.8 us
  other arithmetic: 49 us -> 0 us
  waiting for transfers between devices: 30.3 us -> 0 us
  starting transfers between devices: 24.5 us -> 0 us
  matrix products: 24.4 us -> 0 us
  local copies, waits for them, and re-layouts: 13.9 us -> 3.65 us
  blocking collectives: 6.68 us -> 0 us
    pallas_call x0 -> x1, Pallas kernels: none -> 56.8 us  [body(): pl.pallas_call(functools.partial(kernel, nx, ny, radius, terms), out_shap...]
    eq x66 -> x0, other arithmetic: 32.9 us -> none  [spread_taps(): offsets == position]
    dot_general x35 -> x0, matrix products: 23.6 us -> none  [contract(): return jnp.einsum(formula, left, right, precision=lax.Precision.HIGH)]
    ppermute x8 -> x0, waiting for transfers between devices: 16.6 us -> none  [the longest x4 14.2 us: padded_2(): before = lax.ppermute(last, axis, up)]
    ppermute x8 -> x0, starting transfers between devices: 14.5 us -> none  [the longest x4 11.1 us: padded_2(): after = lax.ppermute(first, axis, down)]
    all_to_all x3 -> x0, waiting for transfers between devices: 13.6 us -> none  [the longest x1 6.39 us: body(): lax.all_to_all(windows, 'gx', split_axis=0, concat_axis=2, tiled=True)[0]]
    all_to_all x3 -> x0, starting transfers between devices: 9.96 us -> none  [the longest x1 3.35 us: body(): lax.all_to_all(turned_yz, 'gx', split_axis=2, concat_axis=1, tiled=True)]
    add x8 -> x0, other arithmetic: 8.61 us -> none  [the longest x6 8.6 us: spread_taps(): table + jnp.where(offsets == position, taps[:, position, None, None], 0.0)]
  transfers between devices with their start and end apart: 11 -> 0, of which waited for: 7 -> 0; matrix products, arithmetic and copies ran while one was open for 42% -> 0% of each run, Pallas kernels for 0% -> 0%
where the time goes in v2:
time: 61.5 us; the launch traced here: 60.5 us
  Pallas kernels  56.8 us (92%)
  local copies, waits for them, and re-layouts  3.65 us (6%)
    pallas_call x1, Pallas kernels, body(): pl.pallas_call(functools.partial(kernel, nx, ny, radius, terms), out_shap...  56.8 us
    unnamed x1, local copies, waits for them, and re-layouts  2.31 us
    reshape x1, local copies, waits for them, and re-layouts, body(): kernel_taps.reshape(-1)  1.34 us

profile of v2, /device:TPU:0, one launch (start us, length us, event | category | flops | bytes accessed | tf_op | source)
XLA Modules:
  0.0 60.5 jit_solution(5445374104789978216)
XLA Ops:
  0.0 1.3 %reshape.3.taps = f32[189]{0:T(256)} reshape(f32[3,3,21]{2,1,0:T(4,128)} %param.11) | data formatting | bytes 1512 | tf_op jit(solution)/shard_map/reshape | solution.py:394
  1.3 56.8 %shard_map.100 = f32[32,32,256]{2,1,0:T(8,128)} custom-call(f32[189]{0:T(256)} %reshape.3.taps, f32[32,32,256]{2,1,0:T(8,128)} %q.1, bf16[24,96]{1,0:T(8,128)(2,1)} %constant.16.clone.ry1, bf16[256,128]{1,0:T(8,128)(2,1)} %constant.17.clone.rz1, bf16[8,48]{1,0:T(8,128)(2,1)} %constant.18.clone.ry2, bf16[128,64]{1,0:T(8,128)(2,1)} %constant.19.clone.rz2, ...), custom_call_target="tpu_custom_call" | custom-call | tf_op jit(solution)/shard_map/pallas_call | solution.py:385
  58.2 2.3 %copy.12 = f32[32,32,256]{2,1,0:T(8,128)} copy(f32[32,32,256]{2,1,0:T(8,128)} %shard_map.100) | data formatting | bytes 2097152

commit v3 on v2

v3 whole, which is shorter than its diff:
```python
import functools

import jax
import jax.numpy as jnp
import numpy as np
from jax import lax
from jax.experimental import pallas as pl
from jax.experimental.pallas import tpu as pltpu
from jax.sharding import PartitionSpec as P

SPLINE = (0.125, 0.5, 0.75, 0.5, 0.125)
F32, BF16 = jnp.float32, jnp.bfloat16
MESH = pl.DeviceIdType.MESH


def spline_at(offset):
    return SPLINE[offset + 2] if -2 <= offset <= 2 else 0.0


def fixed_table(rows, cols, width):
    table = np.zeros((width, len(cols)), np.float32)
    for a, fine in enumerate(rows):
        for b, other in enumerate(cols):
            if fine is not None and other is not None:
                table[a, b] = spline_at(other - 2 * fine)
    return table


def lifted_table(rows, cols, width):
    table = np.zeros((width, len(cols)), np.float32)
    for a, fine in enumerate(rows):
        for b, coarse in enumerate(cols):
            if coarse is not None:
                table[a, b] = spline_at(fine - 2 * coarse)
    return table


def twice(table):
    return jnp.asarray(np.concatenate([table, table], axis=1), BF16)


def halves(value):
    high = value.astype(BF16)
    return high, (value - high.astype(F32)).astype(BF16)


def dot(left, right):
    return jnp.dot(left, right, preferred_element_type=F32)


def stacked2(value):
    high, low = halves(value)
    return jnp.concatenate([high, low], axis=0)


def stacked3(value):
    high, low = halves(value)
    return jnp.concatenate([high, low, high], axis=0)


def repeat(count, step, body):
    def trip(i, carry):
        for k in range(step):
            body(i * step + k)
        return carry

    assert count % step == 0
    lax.fori_loop(0, count // step, trip, 0)


def kernel(nx, ny, radius, terms, taps, q, ry1, rz1, ry2, rz2, uy2, uz2, uy1, uz1, out,
           fine, mid, ext, got, left1, right1, low1, high1, l2w, cols2, seen2, strip2, far2, top,
           ty0, ty1, ty2, tz0, tz1, tz2, y0, s0, y1, s1, y2, s2, r1, l1w, l2y, tx, ty, md, my,
           send, recv):
    bx, by, bz = q.shape
    hx, hy, hz = bx // 2, by // 2, bz // 2
    ex, ey, ez = bx // 4, by // 4, bz // 4
    count = 2 * radius + 1
    margin = radius + 1
    me_x, me_y = lax.axis_index("gx"), lax.axis_index("gy")
    reach = 2
    wy = min(ny, 2 * reach + 1)
    low_y = -((wy - 1) // 2)

    def device(dx, dy):
        return {"gx": lax.rem(me_x + dx + nx, nx), "gy": lax.rem(me_y + dy + ny, ny)}

    peers = {}
    for dx, dy in [(-1, 0), (1, 0), (0, -1), (0, 1), (-2, 0), (2, 0)] + [
        (0, -(low_y + k)) for k in range(wy)
    ]:
        if dx % nx or dy % ny:
            peers[(dx % nx, dy % ny)] = (dx, dy)
    barrier = pltpu.get_barrier_semaphore()
    for dx, dy in peers.values():
        pl.semaphore_signal(barrier, inc=1, device_id=device(dx, dy), device_id_type=MESH)

    def tap(level, member, position):
        return taps[level, member, position]

    def band(level, member, rows, cols, first, cycle, places):
        column = lax.broadcasted_iota(jnp.int32, (rows, cols), 1)
        place = column
        for start, shift in places:
            place = jnp.where(column >= start, column + shift, place)
        offsets = place - lax.broadcasted_iota(jnp.int32, (rows, cols), 0) + first
        if cycle:
            offsets = jnp.where(offsets < 0, offsets + cycle, offsets)
            offsets = jnp.where(offsets >= cycle, offsets - cycle, offsets)
        table = jnp.zeros((rows, cols), F32)
        for position in range(count):
            table = jnp.where(offsets == position, tap(level, member, position), table)
        return table

    def y_table(ref, level, rows, cols, first, cycle, places):
        for member in range(terms):
            high, low = halves(band(level, member, rows, cols, first, cycle, places))
            at = slice(member * rows, (member + 1) * rows)
            ref[at, 0:cols] = high
            ref[at, cols : 2 * cols] = high
            ref[at, 2 * cols : 3 * cols] = low

    def z_table(ref, level, n):
        def rows_of(i):
            start = pl.multiple_of(i * 16, 16)
            offsets = (
                lax.broadcasted_iota(jnp.int32, (16, n), 0)
                + start
                - lax.broadcasted_iota(jnp.int32, (16, n), 1)
                + radius
            )
            offsets = jnp.where(offsets < 0, offsets + n, offsets)
            offsets = jnp.where(offsets >= n, offsets - n, offsets)
            for member in range(terms):
                table = jnp.zeros((16, n), F32)
                for position in range(count):
                    table = jnp.where(offsets == position, tap(level, member, position), table)
                high, low = halves(table)
                ref[member, 0, pl.ds(start, 16), :] = high
                ref[member, 1, pl.ds(start, 16), :] = low

        repeat(n // 16, 1, rows_of)

    sem = [0]

    def remote(source, target, dx, dy):
        index = sem[0]
        sem[0] += 1
        return pltpu.make_async_remote_copy(
            src_ref=source, dst_ref=target, send_sem=send.at[index], recv_sem=recv.at[index],
            device_id=device(dx, dy), device_id_type=MESH,
        )

    def both(copies):
        for copy in copies:
            copy.start()
        return copies

    def arrive(copies):
        for copy in copies:
            copy.wait_recv()

    def weighted(source, i, low, high):
        total = None
        for k in range(-2, 3):
            if low <= 2 * i + k < high:
                piece = source(2 * i + k) * SPLINE[k + 2]
                total = piece if total is None else total + piece
        return total

    rows1, rows2 = hx + 2, ex + 3
    wide1, wide2 = ry1.shape[0], ry2.shape[0]
    for i in range(rows1):
        r1[i] = dot(ry1[...], stacked2(weighted(lambda f: q[f], i - 1, 0, bx)))
    high, low = halves(r1[...].reshape(rows1 * wide1, bz))
    l1w[...] = (dot(high, rz1[...]) + dot(low, rz1[...])).reshape(rows1, wide1, hz)
    for i in range(rows2):
        l2y[i] = dot(ry2[...], stacked2(weighted(lambda f: l1w[f + 1], i - 1, -1, hx + 1)))
    high, low = halves(l2y[...].reshape(rows2 * wide2, hz))
    l2w[...] = (dot(high, rz2[...]) + dot(low, rz2[...])).reshape(rows2, wide2, ez)
    x0, x1 = radius, radius + bx
    extra = radius - 8
    per = 8 // extra
    for i in range(bx):
        g, r = i // per, extra * (i % per)
        ext[0, g, r : r + extra] = q[i, by - radius : by - 8]
        ext[1, g, r : r + extra] = q[i, 8:radius]

    pl.semaphore_wait(barrier, len(peers))
    spot = -low_y
    fan = both([
        remote(l2w, cols2.at[k], 0, -(low_y + k)) for k in range(wy) if low_y + k
    ])
    rim = both([
        remote(l1w.at[rows1 - margin - 1 : rows1], low1, 1, 0),
        remote(l1w.at[0 : margin + 1], high1, -1, 0),
    ])
    g1 = bx // per
    side = both([
        remote(q.at[:, by - 8 : by], fine.at[x0:x1, by : by + 8], 0, 1),
        remote(q.at[:, 0:8], fine.at[x0:x1, by + 8 : by + 16], 0, -1),
        remote(ext.at[0, 0:g1], got.at[0, 0:g1], 0, 1),
        remote(ext.at[1, 0:g1], got.at[1, 0:g1], 0, -1),
    ])
    y_table(ty2, 2, wide2, wy * ey, low_y * ey + 1 + radius, wy * ey if ny <= 2 * reach + 1 else 0, [])
    z_table(tz2, 2, ez)

    cols2[spot] = l2w[...]
    arrive(fan)
    for k in range(wy):
        strip2[:, k * ey : (k + 1) * ey, :] = cols2[k, :, 0:ey, :]
    for k in range(wy):
        for at, place in ((ey, (k + 1) * ey), (ey + 1, (k + 1) * ey + 1), (ey + 2, k * ey - 1)):
            if ny <= 2 * reach + 1:
                place %= wy * ey
            if 0 <= place < wy * ey:
                strip2[:, place : place + 1, :] += cols2[k, :, at : at + 1, :]
    tail = margin - ex + 2
    lines = both([
        remote(strip2, seen2.at[0], 1, 0),
        remote(strip2, seen2.at[1], -1, 0),
        remote(strip2.at[rows2 - tail : rows2], far2.at[0], 2, 0),
        remote(strip2.at[0:tail], far2.at[1], -2, 0),
    ])
    far = both([
        remote(q.at[bx - radius : bx], fine.at[0:x0, 0:by], 1, 0),
        remote(q.at[0:radius], fine.at[x1 : x1 + radius, 0:by], -1, 0),
    ])
    z_table(tz1, 1, hz)

    arrive(rim)
    mid[0 : margin + 1, 0:wide1] = low1[...]
    mid[margin + 1 : margin + hx - 1, 0:wide1] = l1w[2:hx]
    mid[margin + hx - 1 : margin + hx + margin, 0:wide1] = high1[...]
    for i, j in ((margin - 1, 0), (margin, 1), (margin + hx - 1, hx), (margin + hx, hx + 1)):
        mid[i, 0:wide1] += l1w[j]
    left1[...] = mid[:, 1 : hy + 1, :]
    right1[:, 0:1, :] = mid[:, hy + 1 : hy + 2, :]
    right1[:, 1:hy, :] = mid[:, 0 : hy - 1, :]
    rim2 = both([
        remote(left1, mid.at[:, wide1 : wide1 + hy], 0, 1),
        remote(right1, mid.at[:, wide1 + hy : wide1 + 2 * hy], 0, -1),
    ])
    fine[x0:x1, 0:by, :] = q[...]
    y_table(ty0, 0, by, by + 24, radius, 0, [(by, -by - 8), (by + 8, -8), (by + 16, -by - 16 - radius), (by + 16 + extra, -8 - extra), (by + 16 + 2 * extra, 1000)])
    y_table(ty1, 1, wide1, wide1 + 2 * hy, radius + 1, 0, [(hy + 1, -hy - 2), (hy + 2, 1000), (wide1, -wide1 - hy + 1), (wide1 + hy, -wide1 - 1)])
    z_table(tz0, 0, bz)
    spare = jnp.zeros((8 - 2 * extra, bz), F32)

    def unpack(rows, first):
        for n, i in enumerate(rows):
            g, r = first + n // per, extra * (n % per)
            fine[i, by + 16 : by + 16 + extra] = got[0, g, r : r + extra]
            fine[i, by + 16 + extra : by + 16 + 2 * extra] = got[1, g, r : r + extra]
            fine[i, by + 16 + 2 * extra : by + 24] = spare

    outer = list(range(x0)) + list(range(x1, x1 + radius))
    arrive(far)
    for n, i in enumerate(outer):
        g, r = g1 + n // per, extra * (n % per)
        ext[0, g, r : r + extra] = fine[i, by - radius : by - 8, :]
        ext[1, g, r : r + extra] = fine[i, 8:radius, :]
    g2 = ext.shape[1]
    corner = both(
        [remote(fine.at[a:b, by - 8 : by], fine.at[a:b, by : by + 8], 0, 1) for a, b in ((0, x0), (x1, x1 + radius))]
        + [remote(fine.at[a:b, 0:8], fine.at[a:b, by + 8 : by + 16], 0, -1) for a, b in ((0, x0), (x1, x1 + radius))]
        + [remote(ext.at[0, g1:g2], got.at[0, g1:g2], 0, 1), remote(ext.at[1, g1:g2], got.at[1, g1:g2], 0, -1)]
    )

    def correlate_y(ref, source, table, rows, step, first=0):
        width = table.shape[0] // terms

        def one(i):
            i = i + first
            value = dot(table[...], stacked3(source[i]))
            for member in range(terms):
                ref[member, i] = value[member * width : (member + 1) * width]

        repeat(rows, step, one)

    def correlate_x(ref, source, level, rows, first, step):
        def one(i):
            for member in range(terms):
                total = None
                for position in range(count):
                    piece = source[member, i + first + position] * tap(level, member, position)
                    total = piece if total is None else total + piece
                high, low = halves(total)
                ref[member, 0, i] = high
                ref[member, 1, i] = low

        repeat(rows, step, one)

    def correlate_z(ref, table, a, b):
        size = (b - a) * ref.shape[3]
        total = None
        for member in range(terms):
            high = ref[member, 0, a:b].reshape(size, ref.shape[4])
            low = ref[member, 1, a:b].reshape(size, ref.shape[4])
            piece = dot(high, table[member, 0]) + dot(low, table[member, 0]) + dot(high, table[member, 1])
            total = piece if total is None else total + piece
        return total

    def prolong_x(source, j, first):
        at = j - 2 * first
        if j % 2 == 0:
            c = (j // 2) - first
            return source[c - 1] * 0.125 + source[c] * 0.75 + source[c + 1] * 0.125
        c = (j - 1) // 2 - first
        return source[c] * 0.5 + source[c + 1] * 0.5

    arrive(side)
    unpack(range(x0, x1), 0)
    correlate_y(y0, fine, ty0, bx, 4, x0)

    arrive(lines)
    top[...] = jnp.zeros(top.shape, F32)
    home = radius
    for first, source in ((home, strip2), (home - ex, seen2.at[0]), (home + ex, seen2.at[1])):
        top[first : first + rows2] += source[...]
    top[0:tail] += far2[0]
    top[home + 2 * ex : home + 2 * ex + tail] += far2[1]
    correlate_y(y2, top, ty2, top.shape[0], top.shape[0])
    correlate_x(s2, y2, 2, rows2, 0, 1)
    tx[...] = correlate_z(s2, tz2, 0, rows2).reshape(tx.shape)
    for j in range(hx + 2):
        ty[j] = dot(uy2[...], stacked2(prolong_x(tx, j - 1, -1)))
    high, low = halves(ty[...].reshape((hx + 2) * ty.shape[1], ez))
    lifted = dot(high, uz2[...]) + dot(low, uz2[...])

    md[...] = lifted.reshape(md.shape)
    arrive(rim2)
    correlate_y(y1, mid, ty1, hx + 2 * margin, 2)
    correlate_x(s1, y1, 1, hx + 2, 0, 1)
    md[...] += correlate_z(s1, tz1, 0, hx + 2).reshape(md.shape)
    for j in range(bx):
        high, low = halves(dot(uy1[...], stacked2(prolong_x(md, j, -1))))
        my[0, j] = high
        my[1, j] = low

    arrive(corner)
    unpack(outer, g1)
    correlate_y(y0, fine, ty0, x0, 5)
    correlate_y(y0, fine, ty0, radius, 5, x1)
    correlate_x(s0, y0, 0, bx, 0, 1)
    for a in range(0, bx, 8):
        total = correlate_z(s0, tz0, a, a + 8)
        high = my[0, a : a + 8].reshape(8 * by, hz)
        low = my[1, a : a + 8].reshape(8 * by, hz)
        total = total + dot(high, uz1[...]) + dot(low, uz1[...])
        out[a : a + 8] = total.reshape(8, by, bz)
    for copy in fan + rim + side + lines + far + rim2 + corner:
        copy.wait_send()


def cyclic_restrict(n):
    rows = np.arange(n)[:, None]
    cols = np.arange(n // 2)[None, :]
    table = np.zeros((n, n // 2), np.float32)
    for k in range(-2, 3):
        table += SPLINE[k + 2] * ((2 * cols + k) % n == rows)
    return table


def body(charges, kernel_taps):
    nx, ny = lax.axis_size("gx"), lax.axis_size("gy")
    levels, terms, count = kernel_taps.shape
    radius = count // 2
    margin = radius + 1
    bx, by, bz = charges.shape
    hx, hy, hz = bx // 2, by // 2, bz // 2
    ex, ey, ez = bx // 4, by // 4, bz // 4
    pad = 16
    wy = min(ny, 5)
    order1 = list(range(hy)) + [hy, -1] + [None] * 6
    ry1 = fixed_table(order1, list(range(by)), len(order1))
    order2 = list(range(ey)) + [ey, ey + 1, -1] + [None] * 5
    ry2 = fixed_table(order2, order1, len(order2))
    rz1, rz2 = cyclic_restrict(bz), cyclic_restrict(hz)
    wide1 = hy + 8
    wide2 = ey + 8
    uy2 = lifted_table(list(range(-1, hy + 1)), list(range(-1, ey + 2)) + [None] * (wide2 - ey - 3), wide1)
    uy1 = lifted_table(list(range(by)), list(range(-1, hy + 1)) + [None] * (wide1 - hy - 2), by)
    fixed = [twice(ry1), jnp.asarray(rz1, BF16), twice(ry2), jnp.asarray(rz2, BF16), twice(uy2),
             jnp.asarray(rz2.T, BF16), twice(uy1), jnp.asarray(rz1.T, BF16)]
    rows1, rows2 = hx + 2, ex + 3
    extra = radius - 8
    packed = -(-(bx + 2 * radius) * extra // 8)
    scratch = [
        pltpu.VMEM(shape, dtype)
        for shape, dtype in (
            ((bx + 2 * radius, by + 24, bz), F32),
            ((hx + 2 * margin, wide1 + 2 * hy, hz), F32),
            ((2, packed, 8, bz), F32),
            ((2, packed, 8, bz), F32),
            ((hx + 2 * margin, hy, hz), F32),
            ((hx + 2 * margin, hy, hz), F32),
            ((margin + 1, wide1, hz), F32),
            ((margin + 1, wide1, hz), F32),
            ((rows2, wide2, ez), F32),
            ((wy, rows2, wide2, ez), F32),
            ((2, rows2, wy * ey, ez), F32),
            ((rows2, wy * ey, ez), F32),
            ((2, margin - ex + 2, wy * ey, ez), F32),
            ((rows2 + 2 * radius, wy * ey, ez), F32),
            ((terms * by, 3 * (by + 24)), BF16),
            ((terms * wide1, 3 * (wide1 + 2 * hy)), BF16),
            ((terms * wide2, 3 * wy * ey), BF16),
            ((terms, 2, bz, bz), BF16),
            ((terms, 2, hz, hz), BF16),
            ((terms, 2, ez, ez), BF16),
            ((terms, bx + 2 * radius, by, bz), F32),
            ((terms, 2, bx, by, bz), BF16),
            ((terms, hx + 2 * margin, wide1, hz), F32),
            ((terms, 2, hx + 2, wide1, hz), BF16),
            ((terms, rows2 + 2 * radius, wide2, ez), F32),
            ((terms, 2, rows2, wide2, ez), BF16),
            ((rows1, wide1, bz), F32),
            ((rows1, wide1, hz), F32),
            ((rows2, wide2, hz), F32),
            ((rows2, wide2, ez), F32),
            ((hx + 2, wide1, ez), F32),
            ((hx + 2, wide1, hz), F32),
            ((2, bx, by, hz), BF16),
        )
    ] + [
        pltpu.SemaphoreType.DMA((48,)),
        pltpu.SemaphoreType.DMA((48,)),
    ]
    return pl.pallas_call(
        functools.partial(kernel, nx, ny, radius, terms),
        out_shape=jax.ShapeDtypeStruct(charges.shape, F32),
        in_specs=[pl.BlockSpec(memory_space=pltpu.SMEM)] + [pl.BlockSpec(memory_space=pltpu.VMEM)] * 9,
        out_specs=pl.BlockSpec(memory_space=pltpu.VMEM),
        scratch_shapes=scratch,
        compiler_params=pltpu.CompilerParams(
            collective_id=0, has_side_effects=True, vmem_limit_bytes=60 * 2**20
        ),
    )(kernel_taps, charges, *fixed)


def solution(mesh):
    return jax.shard_map(
        body,
        mesh=mesh,
        in_specs=(P("gx", "gy", None), P()),
        out_specs=P("gx", "gy", None),
        check_vma=False,
    )
```

time: 61.5 us -> 58 us (0.943); the launches traced: 60.5 us -> 57.8 us
  local copies, waits for them, and re-layouts: 3.65 us -> 2.31 us
  Pallas kernels: 56.8 us -> 55.5 us
    reshape x1 -> x0, local copies, waits for them, and re-layouts: 1.34 us -> none  [body(): kernel_taps.reshape(-1)]
    pallas_call x1, Pallas kernels: 56.8 us -> 55.5 us  [body(): pl.pallas_call(functools.partial(kernel, nx, ny, radius, terms), out_shap...]
where the time goes in v3:
time: 58 us; the launch traced here: 57.8 us
  Pallas kernels  55.5 us (96%)
  local copies, waits for them, and re-layouts  2.31 us (4%)
    pallas_call x1, Pallas kernels, body(): pl.pallas_call(functools.partial(kernel, nx, ny, radius, terms), out_shap...  55.5 us
    unnamed x1, local copies, waits for them, and re-layouts  2.31 us

profile of v3, /device:TPU:0, one launch (start us, length us, event | category | flops | bytes accessed | tf_op | source)
XLA Modules:
  0.0 57.8 jit_solution(6185818822057582477)
XLA Ops:
  0.0 55.5 %shard_map.100 = f32[32,32,256]{2,1,0:T(8,128)} custom-call(f32[3,3,21]{2,1,0:T(4,128)} %taps.1, f32[32,32,256]{2,1,0:T(8,128)} %q.1, bf16[24,64]{1,0:T(8,128)(2,1)} %constant.16.clone.ry1, bf16[256,128]{1,0:T(8,128)(2,1)} %constant.17.clone.rz1, bf16[16,48]{1,0:T(8,128)(2,1)} %constant.18.clone.ry2, bf16[128,64]{1,0:T(8,128)(2,1)} %constant.19.clone.rz2, ...), custom_call_target="tpu_custom_call" | custom-call | tf_op jit(solution)/shard_map/pallas_call | solution.py:430
  55.5 2.3 %copy.12 = f32[32,32,256]{2,1,0:T(8,128)} copy(f32[32,32,256]{2,1,0:T(8,128)} %shard_map.100) | data formatting | bytes 2097152

commit v4 on v3

--- a/solution.py
+++ b/solution.py
@@ -136,8 +136,8 @@
                 for position in range(count):
                     table = jnp.where(offsets == position, tap(level, member, position), table)
                 high, low = halves(table)
-                ref[member, 0, pl.ds(start, 16), :] = high
-                ref[member, 1, pl.ds(start, 16), :] = low
+                ref[0, pl.ds(pl.multiple_of(member * n + start, 16), 16), :] = high
+                ref[1, pl.ds(pl.multiple_of(member * n + start, 16), 16), :] = low
 
         repeat(n // 16, 1, rows_of)
 
@@ -160,6 +160,9 @@
         for copy in copies:
             copy.wait_recv()
 
+    x0, x1 = radius, radius + bx
+    extra = radius - 8
+    per = 8 // extra
     def weighted(source, i, low, high):
         total = None
         for k in range(-2, 3):
@@ -178,27 +181,26 @@
         l2y[i] = dot(ry2[...], stacked2(weighted(lambda f: l1w[f + 1], i - 1, -1, hx + 1)))
     high, low = halves(l2y[...].reshape(rows2 * wide2, hz))
     l2w[...] = (dot(high, rz2[...]) + dot(low, rz2[...])).reshape(rows2, wide2, ez)
-    x0, x1 = radius, radius + bx
-    extra = radius - 8
-    per = 8 // extra
+    pl.semaphore_wait(barrier, len(peers))
+    spot = -low_y
+    fan = both([
+        remote(l2w, cols2.at[k], 0, -(low_y + k)) for k in range(wy) if low_y + k
+    ])
+    rim = both([
+        remote(l1w.at[rows1 - margin - 1 : rows1], low1, 1, 0),
+        remote(l1w.at[0 : margin + 1], high1, -1, 0),
+    ])
+    g1 = bx // per
+    side = both([
+        remote(q.at[:, by - 8 : by], fine.at[x0:x1, by : by + 8], 0, 1),
+        remote(q.at[:, 0:8], fine.at[x0:x1, by + 8 : by + 16], 0, -1),
+    ])
     for i in range(bx):
         g, r = i // per, extra * (i % per)
         ext[0, g, r : r + extra] = q[i, by - radius : by - 8]
         ext[1, g, r : r + extra] = q[i, 8:radius]
 
-    pl.semaphore_wait(barrier, len(peers))
-    spot = -low_y
-    fan = both([
-        remote(l2w, cols2.at[k], 0, -(low_y + k)) for k in range(wy) if low_y + k
-    ])
-    rim = both([
-        remote(l1w.at[rows1 - margin - 1 : rows1], low1, 1, 0),
-        remote(l1w.at[0 : margin + 1], high1, -1, 0),
-    ])
-    g1 = bx // per
-    side = both([
-        remote(q.at[:, by - 8 : by], fine.at[x0:x1, by : by + 8], 0, 1),
-        remote(q.at[:, 0:8], fine.at[x0:x1, by + 8 : by + 16], 0, -1),
+    side += both([
         remote(ext.at[0, 0:g1], got.at[0, 0:g1], 0, 1),
         remote(ext.at[1, 0:g1], got.at[1, 0:g1], 0, -1),
     ])
@@ -226,6 +228,19 @@
         remote(q.at[bx - radius : bx], fine.at[0:x0, 0:by], 1, 0),
         remote(q.at[0:radius], fine.at[x1 : x1 + radius, 0:by], -1, 0),
     ])
+    fine[x0:x1, 0:by, :] = q[...]
+    y_table(ty0, 0, by, by + 24, radius, 0, [(by, -by - 8), (by + 8, -8), (by + 16, -by - 16 - radius), (by + 16 + extra, -8 - extra), (by + 16 + 2 * extra, 1000)])
+    y_table(ty1, 1, wide1, wide1 + 2 * hy, radius + 1, 0, [(hy + 1, -hy - 2), (hy + 2, 1000), (wide1, -wide1 - hy + 1), (wide1 + hy, -wide1 - 1)])
+    z_table(tz0, 0, bz)
+    spare = jnp.zeros((8 - 2 * extra, bz), F32)
+
+    def unpack(rows, first):
+        for n, i in enumerate(rows):
+            g, r = first + n // per, extra * (n % per)
+            fine[i, by + 16 : by + 16 + extra] = got[0, g, r : r + extra]
+            fine[i, by + 16 + extra : by + 16 + 2 * extra] = got[1, g, r : r + extra]
+            fine[i, by + 16 + 2 * extra : by + 24] = spare
+
     z_table(tz1, 1, hz)
 
     arrive(rim)
@@ -241,32 +256,7 @@
         remote(left1, mid.at[:, wide1 : wide1 + hy], 0, 1),
         remote(right1, mid.at[:, wide1 + hy : wide1 + 2 * hy], 0, -1),
     ])
-    fine[x0:x1, 0:by, :] = q[...]
-    y_table(ty0, 0, by, by + 24, radius, 0, [(by, -by - 8), (by + 8, -8), (by + 16, -by - 16 - radius), (by + 16 + extra, -8 - extra), (by + 16 + 2 * extra, 1000)])
-    y_table(ty1, 1, wide1, wide1 + 2 * hy, radius + 1, 0, [(hy + 1, -hy - 2), (hy + 2, 1000), (wide1, -wide1 - hy + 1), (wide1 + hy, -wide1 - 1)])
-    z_table(tz0, 0, bz)
-    spare = jnp.zeros((8 - 2 * extra, bz), F32)
-
-    def unpack(rows, first):
-        for n, i in enumerate(rows):
-            g, r = first + n // per, extra * (n % per)
-            fine[i, by + 16 : by + 16 + extra] = got[0, g, r : r + extra]
-            fine[i, by + 16 + extra : by + 16 + 2 * extra] = got[1, g, r : r + extra]
-            fine[i, by + 16 + 2 * extra : by + 24] = spare
-
     outer = list(range(x0)) + list(range(x1, x1 + radius))
-    arrive(far)
-    for n, i in enumerate(outer):
-        g, r = g1 + n // per, extra * (n % per)
-        ext[0, g, r : r + extra] = fine[i, by - radius : by - 8, :]
-        ext[1, g, r : r + extra] = fine[i, 8:radius, :]
-    g2 = ext.shape[1]
-    corner = both(
-        [remote(fine.at[a:b, by - 8 : by], fine.at[a:b, by : by + 8], 0, 1) for a, b in ((0, x0), (x1, x1 + radius))]
-        + [remote(fine.at[a:b, 0:8], fine.at[a:b, by + 8 : by + 16], 0, -1) for a, b in ((0, x0), (x1, x1 + radius))]
-        + [remote(ext.at[0, g1:g2], got.at[0, g1:g2], 0, 1), remote(ext.at[1, g1:g2], got.at[1, g1:g2], 0, -1)]
-    )
-
     def correlate_y(ref, source, table, rows, step, first=0):
         width = table.shape[0] // terms
 
@@ -278,28 +268,26 @@
 
         repeat(rows, step, one)
 
-    def correlate_x(ref, source, level, rows, first, step):
+    def correlate_x(ref, source, level, rows, first, step, start=0):
         def one(i):
+            i = i + start
             for member in range(terms):
                 total = None
                 for position in range(count):
                     piece = source[member, i + first + position] * tap(level, member, position)
                     total = piece if total is None else total + piece
                 high, low = halves(total)
-                ref[member, 0, i] = high
-                ref[member, 1, i] = low
+                at = slice(member * total.shape[1], (member + 1) * total.shape[1])
+                ref[0, i, :, at] = high
+                ref[1, i, :, at] = low
 
         repeat(rows, step, one)
 
     def correlate_z(ref, table, a, b):
-        size = (b - a) * ref.shape[3]
-        total = None
-        for member in range(terms):
-            high = ref[member, 0, a:b].reshape(size, ref.shape[4])
-            low = ref[member, 1, a:b].reshape(size, ref.shape[4])
-            piece = dot(high, table[member, 0]) + dot(low, table[member, 0]) + dot(high, table[member, 1])
-            total = piece if total is None else total + piece
-        return total
+        size = (b - a) * ref.shape[2]
+        high = ref[0, a:b].reshape(size, ref.shape[3])
+        low = ref[1, a:b].reshape(size, ref.shape[3])
+        return dot(high, table[0]) + dot(low, table[0]) + dot(high, table[1])
 
     def prolong_x(source, j, first):
         at = j - 2 * first
@@ -338,17 +326,34 @@
         my[0, j] = high
         my[1, j] = low
 
+    def finish(a, b):
+        high = my[0, a:b].reshape((b - a) * by, hz)
+        low = my[1, a:b].reshape((b - a) * by, hz)
+        total = correlate_z(s0, tz0, a, b) + dot(high, uz1[...]) + dot(low, uz1[...])
+        out[a:b] = total.reshape(b - a, by, bz)
+
+    correlate_x(s0, y0, 0, bx - 2 * radius, 0, 1, radius)
+    finish(radius, bx - radius)
+    arrive(far)
+    for n, i in enumerate(outer):
+        g, r = g1 + n // per, extra * (n % per)
+        ext[0, g, r : r + extra] = fine[i, by - radius : by - 8, :]
+        ext[1, g, r : r + extra] = fine[i, 8:radius, :]
+    g2 = ext.shape[1]
+    corner = both(
+        [remote(fine.at[a:b, by - 8 : by], fine.at[a:b, by : by + 8], 0, 1) for a, b in ((0, x0), (x1, x1 + radius))]
+        + [remote(fine.at[a:b, 0:8], fine.at[a:b, by + 8 : by + 16], 0, -1) for a, b in ((0, x0), (x1, x1 + radius))]
+        + [remote(ext.at[0, g1:g2], got.at[0, g1:g2], 0, 1), remote(ext.at[1, g1:g2], got.at[1, g1:g2], 0, -1)]
+    )
+
     arrive(corner)
     unpack(outer, g1)
     correlate_y(y0, fine, ty0, x0, 5)
     correlate_y(y0, fine, ty0, radius, 5, x1)
-    correlate_x(s0, y0, 0, bx, 0, 1)
-    for a in range(0, bx, 8):
-        total = correlate_z(s0, tz0, a, a + 8)
-        high = my[0, a : a + 8].reshape(8 * by, hz)
-        low = my[1, a : a + 8].reshape(8 * by, hz)
-        total = total + dot(high, uz1[...]) + dot(low, uz1[...])
-        out[a : a + 8] = total.reshape(8, by, bz)
+    correlate_x(s0, y0, 0, radius, 0, 1)
+    correlate_x(s0, y0, 0, radius, 0, 1, bx - radius)
+    finish(0, radius)
+    finish(bx - radius, bx)
     for copy in fan + rim + side + lines + far + rim2 + corner:
         copy.wait_send()
 
@@ -406,15 +411,15 @@
             ((terms * by, 3 * (by + 24)), BF16),
             ((terms * wide1, 3 * (wide1 + 2 * hy)), BF16),
             ((terms * wide2, 3 * wy * ey), BF16),
-            ((terms, 2, bz, bz), BF16),
-            ((terms, 2, hz, hz), BF16),
-            ((terms, 2, ez, ez), BF16),
+            ((2, terms * bz, bz), BF16),
+            ((2, terms * hz, hz), BF16),
+            ((2, terms * ez, ez), BF16),
             ((terms, bx + 2 * radius, by, bz), F32),
-            ((terms, 2, bx, by, bz), BF16),
+            ((2, bx, by, terms * bz), BF16),
             ((terms, hx + 2 * margin, wide1, hz), F32),
-            ((terms, 2, hx + 2, wide1, hz), BF16),
+            ((2, hx + 2, wide1, terms * hz), BF16),
             ((terms, rows2 + 2 * radius, wide2, ez), F32),
-            ((terms, 2, rows2, wide2, ez), BF16),
+            ((2, rows2, wide2, terms * ez), BF16),
             ((rows1, wide1, bz), F32),
             ((rows1, wide1, hz), F32),
             ((rows2, wide2, hz), F32),

time: 58 us -> 55.2 us (0.952)
  the two profiles are of different devices: /device:TPU:0 before, /device:TPU:1 now
where the time goes in v4:
time: 55.2 us; the launch traced here: 55 us
  Pallas kernels  52.7 us (95%)
  local copies, waits for them, and re-layouts  2.31 us (4%)
    pallas_call x1, Pallas kernels, body(): pl.pallas_call(functools.partial(kernel, nx, ny, radius, terms), out_shap...  52.7 us
    unnamed x1, local copies, waits for them, and re-layouts  2.31 us

profile of v4, /device:TPU:1, one launch (start us, length us, event | category | flops | bytes accessed | tf_op | source)
XLA Modules:
  0.0 55.0 jit_solution(12701041701118754324)
XLA Ops:
  0.0 52.7 %shard_map.100 = f32[32,32,256]{2,1,0:T(8,128)} custom-call(f32[3,3,21]{2,1,0:T(4,128)} %taps.1, f32[32,32,256]{2,1,0:T(8,128)} %q.1, bf16[24,64]{1,0:T(8,128)(2,1)} %constant.16.clone.ry1, bf16[256,128]{1,0:T(8,128)(2,1)} %constant.17.clone.rz1, bf16[16,48]{1,0:T(8,128)(2,1)} %constant.18.clone.ry2, bf16[128,64]{1,0:T(8,128)(2,1)} %constant.19.clone.rz2, ...), custom_call_target="tpu_custom_call" | custom-call | tf_op jit(solution)/shard_map/pallas_call | solution.py:435
  52.7 2.3 %copy.12 = f32[32,32,256]{2,1,0:T(8,128)} copy(f32[32,32,256]{2,1,0:T(8,128)} %shard_map.100) | data formatting | bytes 2097152
